TPU v7x, 512 devices: a whole 4x4x16 slice. The times are simulated.
512 devices in a mesh: req: 128 (over z, y, core), tp: 4 (over x).
Axes of the slice: x: 4, y: 4, z: 16, core: 2. Of those that a mesh axis runs over, the one named last changes fastest.
Arguments:
- query: bfloat16 [512, 2048], P('req', 'tp'), may hold values from -8 to 8
- key_new: bfloat16 [512, 2048], P('req', 'tp'), may hold values from -4 to 4
- value_new: bfloat16 [512, 2048], P('req', 'tp'), may hold values from -4 to 4
- resid: bfloat16 [512, 2048], P('req', 'tp'), may hold values from -6 to 6
- lengths: int32 [512], replicated, may hold values from 1 to 512, as said below
- owner: int32 [512], replicated, may hold values from 0 to 127, as said below
- page_table: int32 [512, 16], replicated, may hold values from 0 to 21, as said below
- kv_pool: bfloat16 [2, 2816, 32, 2048], P(None, 'req', None, 'tp'), may hold values from -4 to 4
- out_weight: bfloat16 [2048, 2048], P('tp'), may hold values from -0.125 to 0.125
- out_bias: bfloat16 [2048], P('tp'), may hold values from -3 to 3
- norm_gain: bfloat16 [2048], P('tp'), may hold values from 0.099609375 to 1.8984375
- norm_bias: bfloat16 [2048], P('tp'), may hold values from -3 to 3
- up_weight_t: bfloat16 [8192, 2048], P('req', 'tp'), may hold values from -0.125 to 0.125
- up_bias: bfloat16 [8192], P('req'), may hold values from -3 to 3
- down_weight: bfloat16 [8192, 2048], P('req', 'tp'), may hold values from -0.0625 to 0.0625
- down_bias: bfloat16 [2048], P('tp'), may hold values from -3 to 3
- order: int32 [512], replicated, may hold values from 0 to 511, each once
Outputs:
- layer_out: bfloat16 [512, 2048], P('req', 'tp')
Inputs may be any that keep to these rules, and one draw needn't show every extreme that they name: `lengths`: one request in 32 (at least one) is long, with a length from 256 to 512; the others have at most 63 positions. `owner`: every index of req owns exactly 4 requests, at most one of them long, and no two of them among the 4 rows that one index of req holds. `page_table`: entry j of request r for j < ceil(lengths[r] / 32) names a page of the owner's pool that no other entry of that owner's requests below that bound names; later entries are arbitrary pages.
All inputs are finite; a program needn't handle non-finite values.
Results may differ from a plain program's by a relative error of at most 0.015.
Values may be sent and summed in bfloat16 or wider, within the bound.
A program may use at most 64 MiB of HBM per device.

v0:
```python
import math

import jax
import jax.numpy as jnp
from jax import lax
from jax.sharding import PartitionSpec as P

D = 2048
HEAD_DIM = 128


norm_eps = 1e-05


def per_device(
    query,
    key_new,
    value_new,
    resid,
    lengths,
    owner,
    page_table,
    kv_pool,
    out_weight,
    out_bias,
    norm_gain,
    norm_bias,
    up_weight_t,
    up_bias,
    down_weight,
    down_bias,
    order,
):
    owned_count = query.shape[0]
    local_heads = query.shape[1] // HEAD_DIM
    pool_pages = kv_pool.shape[1]
    page_len = kv_pool.shape[2]
    max_pages = page_table.shape[1]
    request_count = lengths.shape[0]
    devices = lax.axis_size("req")
    device_index = lax.axis_index("req")
    score_scale = 1.0 / math.sqrt(HEAD_DIM)
    highest = lax.Precision.HIGHEST
    owner_hot = (owner[:, None] == jnp.arange(devices, dtype=jnp.int32)[None, :]).astype(jnp.int32)
    owner_rank = jnp.sum((jnp.cumsum(owner_hot, axis=0) - 1) * owner_hot, axis=1)
    slot_pos = owner * owned_count + owner_rank
    picker = (owner[None, :] == device_index) & (
        owner_rank[None, :] == jnp.arange(owned_count, dtype=jnp.int32)[:, None]
    )
    own_ids = jnp.sum(
        picker.astype(jnp.int32) * jnp.arange(request_count, dtype=jnp.int32)[None, :], axis=1
    )
    query_all, key_all, value_all, resid_all = (
        lax.all_gather(query, "req", axis=0, tiled=True),
        lax.all_gather(key_new, "req", axis=0, tiled=True),
        lax.all_gather(value_new, "req", axis=0, tiled=True),
        lax.all_gather(resid, "req", axis=0, tiled=True),
    )
    pick_matrix = picker.astype(jnp.bfloat16)

    def pick_rows(source_rows):
        return jnp.dot(pick_matrix, source_rows, preferred_element_type=jnp.float32).astype(
            jnp.bfloat16
        )

    query_own = pick_rows(query_all)
    key_own = pick_rows(key_all)
    value_own = pick_rows(value_all)
    resid_own = pick_rows(resid_all)
    own_len = lengths[own_ids]
    own_table = page_table[own_ids]
    own_pages = (own_len + page_len - 1) // page_len
    page_used = jnp.arange(max_pages, dtype=jnp.int32)[None, :] < own_pages[:, None]
    page_match = (
        own_table[:, :, None] == jnp.arange(pool_pages, dtype=jnp.int32)[None, None, :]
    ) & page_used[:, :, None]
    page_hot = jnp.any(page_match, axis=1).T
    page_index = jnp.sum(
        page_match.astype(jnp.int32) * jnp.arange(max_pages, dtype=jnp.int32)[None, :, None],
        axis=(0, 1),
    )
    page_limit = jnp.sum(page_hot.astype(jnp.int32) * own_len[None, :], axis=1)
    query_page = jnp.dot(
        page_hot.astype(jnp.bfloat16), query_own, preferred_element_type=jnp.float32
    ).astype(jnp.bfloat16)
    query_page = query_page.reshape(pool_pages, local_heads, HEAD_DIM)
    page_keys = kv_pool[0].reshape(pool_pages, page_len, local_heads, HEAD_DIM)
    page_values = kv_pool[1].reshape(pool_pages, page_len, local_heads, HEAD_DIM)
    scores = (
        jnp.einsum("phd,pthd->pht", query_page, page_keys, preferred_element_type=jnp.float32)
        * score_scale
    )
    position = page_index[:, None] * page_len + jnp.arange(page_len, dtype=jnp.int32)[None, :]
    valid_mask = (position < page_limit[:, None])[:, None, :]
    scores = jnp.where(valid_mask, scores, -jnp.inf)
    query_heads = query_own.astype(jnp.float32).reshape(owned_count, local_heads, HEAD_DIM)
    key_heads = key_own.astype(jnp.float32).reshape(owned_count, local_heads, HEAD_DIM)
    self_score = jnp.sum(query_heads * key_heads, axis=-1) * score_scale
    page_top = jnp.max(scores, axis=2)
    slot_top = jnp.max(jnp.where(page_hot[:, :, None], page_top[:, None, :], -jnp.inf), axis=0)
    slot_top = jnp.maximum(slot_top, self_score)
    page_ref = jnp.sum(jnp.where(page_hot[:, :, None], slot_top[None, :, :], 0.0), axis=1)
    weights = jnp.where(valid_mask, jnp.exp(scores - page_ref[:, :, None]), 0.0)
    page_total = jnp.sum(weights, axis=2)
    self_weight = jnp.exp(self_score - slot_top)
    slot_total = (
        jnp.sum(jnp.where(page_hot[:, :, None], page_total[:, None, :], 0.0), axis=0) + self_weight
    )
    page_numer = jnp.einsum(
        "pht,pthd->phd",
        weights.astype(jnp.bfloat16),
        page_values,
        preferred_element_type=jnp.float32,
    )
    slot_numer = jnp.einsum(
        "pr,phd->rhd", page_hot.astype(jnp.float32), page_numer, precision=highest
    )
    value_heads = value_own.astype(jnp.float32).reshape(owned_count, local_heads, HEAD_DIM)
    slot_numer = (
        slot_numer + self_weight.astype(jnp.bfloat16).astype(jnp.float32)[:, :, None] * value_heads
    )
    attn = (
        (slot_numer / slot_total[:, :, None])
        .astype(jnp.bfloat16)
        .reshape(owned_count, local_heads * HEAD_DIM)
    )
    projected = lax.psum_scatter(
        lax.dot_general(
            out_weight, attn, (((0,), (1,)), ((), ())), preferred_element_type=jnp.float32
        ),
        "tp",
        scatter_dimension=0,
        tiled=True,
    )
    bias_row = out_bias.astype(jnp.float32)[None, :]
    stream_own = (resid_own.astype(jnp.float32) + projected.T + bias_row).astype(jnp.bfloat16)
    own_f = stream_own.astype(jnp.float32)
    row_sum, row_square = lax.psum((jnp.sum(own_f, axis=1), jnp.sum(own_f * own_f, axis=1)), "tp")
    mean_own = row_sum / D
    inverse_own = lax.rsqrt(row_square / D - mean_own * mean_own + norm_eps)
    stream_all = lax.all_gather(stream_own, "req", axis=0, tiled=True)
    mean_all, inverse_all = (
        lax.all_gather(mean_own, "req", axis=0, tiled=True),
        lax.all_gather(inverse_own, "req", axis=0, tiled=True),
    )
    stream_f = stream_all.astype(jnp.float32)
    normed = (
        (stream_f - mean_all[:, None])
        * inverse_all[:, None]
        * norm_gain.astype(jnp.float32)[None, :]
        + norm_bias.astype(jnp.float32)[None, :]
    ).astype(jnp.bfloat16)
    partial_value = lax.dot_general(
        up_weight_t, normed, (((1,), (1,)), ((), ())), preferred_element_type=jnp.float32
    )
    bias_col = up_bias.astype(jnp.float32)[:, None]
    summed = lax.psum(partial_value.astype(jnp.bfloat16), "tp").astype(jnp.float32)
    activated = jax.nn.gelu(summed + bias_col, approximate=False).astype(jnp.bfloat16)
    activated_out = jnp.take(activated, slot_pos[order], axis=1)
    feed_rows = lax.psum_scatter(
        lax.dot_general(
            activated_out, down_weight, (((0,), (0,)), ((), ())), preferred_element_type=jnp.float32
        ),
        "req",
        scatter_dimension=0,
        tiled=True,
    )
    order_mine = lax.dynamic_slice_in_dim(order, device_index * owned_count, owned_count)
    residual_rows = jnp.take(stream_all, slot_pos[order_mine], axis=0)
    combined = (
        residual_rows.astype(jnp.float32) + feed_rows + down_bias.astype(jnp.float32)[None, :]
    )
    return combined.astype(jnp.bfloat16)


def solution(mesh):
    in_specs = (
        P("req", "tp"),
        P("req", "tp"),
        P("req", "tp"),
        P("req", "tp"),
        P(),
        P(),
        P(),
        P(None, "req", None, "tp"),
        P("tp", None),
        P("tp"),
        P("tp"),
        P("tp"),
        P("req", "tp"),
        P("req"),
        P("req", "tp"),
        P("tp"),
        P(),
    )
    out_specs = P("req", "tp")
    return jax.shard_map(
        per_device, mesh=mesh, in_specs=in_specs, out_specs=out_specs, check_vma=False
    )
```

profile of v0, /device:TPU:1, one launch (start us, length us, event | category | flops | bytes accessed | tf_op | source)
XLA Modules:
  0.0 1110.8 jit_solution(9901141611256359280)
XLA Ops:
  6.6 0.9 copy.35
  12.3 91.2 %all-gather.1 = bf16[128,4,512]{2,1,0:T(4,128)(2,1)S(1)} all-gather(bf16[1,4,512]{2,1,0:T(4,128)(2,1)S(1)} %bitcast.78), channel_id=1, replica_groups=mesh['req'=128,'tp'=4] {'req'}, dimensions={0}, use_global_device_ids=true | all-gather | bytes 528384 | tf_op jit(solution)/shard_map/all_gather | solution.py:54
  104.7 1.4 fusion.62
  106.2 1.0 reshape_squeeze.6
  107.9 1.6 fusion.15
  109.7 87.8 %all-gather.2 = bf16[128,4,512]{2,1,0:T(4,128)(2,1)} all-gather(bf16[1,4,512]{2,1,0:T(4,128)(2,1)} %bitcast.79), channel_id=1, replica_groups=mesh['req'=128,'tp'=4] {'req'}, dimensions={0}, use_global_device_ids=true | all-gather | bytes 528384 | tf_op jit(solution)/shard_map/all_gather | solution.py:55
  197.5 1.2 reshape.260
  199.4 1.0 reshape_squeeze.7
  200.7 81.1 %all-gather.3 = bf16[128,4,512]{2,1,0:T(4,128)(2,1)S(1)} all-gather(bf16[1,4,512]{2,1,0:T(4,128)(2,1)S(1)} %bitcast.80), channel_id=1, replica_groups=mesh['req'=128,'tp'=4] {'req'}, dimensions={0}, use_global_device_ids=true | all-gather | bytes 528384 | tf_op jit(solution)/shard_map/all_gather | solution.py:56
  282.0 1.4 fusion.13
  284.2 1.4 copy.50
  285.7 81.7 %all-gather = bf16[128,4,512]{2,1,0:T(4,128)(2,1)S(1)} all-gather(bf16[1,4,512]{2,1,0:T(4,128)(2,1)S(1)} %bitcast.81), channel_id=1, replica_groups=mesh['req'=128,'tp'=4] {'req'}, dimensions={0}, use_global_device_ids=true | all-gather | bytes 528384 | tf_op jit(solution)/shard_map/all_gather | solution.py:57
  367.7 3.5 gather_fusion.4
  373.9 1.1 copy.51
  375.3 80.9 %all-gather.4 = bf16[128,4,512]{2,1,0:T(4,128)(2,1)S(1)} all-gather(bf16[1,4,512]{2,1,0:T(4,128)(2,1)S(1)} %bitcast.73), channel_id=1, replica_groups=mesh['req'=128,'tp'=4] {'req'}, dimensions={0}, use_global_device_ids=true | all-gather | bytes 528384 | tf_op jit(solution)/shard_map/all_gather | solution.py:141
  456.3 8.5 all-reduce.4
  465.0 248.3 %all-reduce.3 = (f32[512]{0:T(512)S(1)}, f32[512]{0:T(512)S(1)}) all-reduce(f32[512]{0:T(512)S(1)} %rsqrt_dynamic-update-slice_fusion, f32[512]{0:T(512)S(1)} %multiply_dynamic-update-slice_fusion), channel_id=1, replica_groups=mesh['req'=128,'tp'=4] {'req'}, use_global_device_ids=true, to_apply=%add.1 | all-reduce | flops 1024 | bytes 8192
  713.3 1.1 fusion
  714.5 47.3 %all-reduce.8.cloned.1.call-done = bf16[64,512]{1,0:T(8,128)(2,1)} async-done(((bf16[64,512]{1,0:T(8,128)(2,1)}), bf16[64,512]{1,0:T(8,128)(2,1)}) %all-reduce.8.cloned.1.call-update) | async-done | bytes 65552 | tf_op jit(solution)/shard_map/psum | solution.py:157
  761.8 1.2 fusion.26
  763.1 1.3 gather_fusion.5
  764.5 1.4 fusion.27
  766.5 336.4 %all-reduce.10.cloned.1.call-done = f32[512,512]{1,0:T(8,128)} async-done(((f32[512,512]{1,0:T(8,128)}), f32[512,512]{1,0:T(8,128)}) %all-reduce.10.cloned.1.call-update) | async-done | bytes 1048592
  1102.9 1.4 fusion.51
  (110 shorter events, 11.9 us)
Async XLA Ops:
  6.5 277.2 %copy-start = (bf16[512,2048]{1,0:T(8,128)(2,1)S(1)}, bf16[512,2048]{1,0:T(8,128)(2,1)}, u32[]{:S(2)}) copy-start(bf16[512,2048]{1,0:T(8,128)(2,1)} %param.25) | copy-start | bytes 6291460
  6.5 3.1 copy-start.1
  6.5 3.8 copy-start.4
  6.5 5.8 copy-start.5
  6.5 367.3 %reduce-scatter.4.cloned.1.call-start = ((), (), s32[]{:S(2)}) async-start(), calls=%async_computation.2 | async-start | bytes 1310720
  109.5 91.2 %copy-start.6 = (bf16[4,512]{1,0:T(4,128)(2,1)S(1)}, bf16[4,512]{1,0:T(4,128)(2,1)}, u32[]{:S(2)}) copy-start(bf16[4,512]{1,0:T(4,128)(2,1)} %param.19) | copy-start | bytes 12292
  283.8 1.9 copy-start.3
  283.8 1.9 copy-start.7
  284.2 83.4 %copy-start.9 = (bf16[512]{0:T(512)(128)(2,1)S(1)}, bf16[512]{0:T(512)(128)(2,1)}, u32[]{:S(2)}) copy-start(bf16[512]{0:T(512)(128)(2,1)} %param.26) | copy-start | bytes 3076
  284.2 83.4 %copy-start.10 = (bf16[512]{0:T(512)(128)(2,1)S(1)}, bf16[512]{0:T(512)(128)(2,1)}, u32[]{:S(2)}) copy-start(bf16[512]{0:T(512)(128)(2,1)} %param.27) | copy-start | bytes 3076
  284.2 83.4 %copy-start.11 = (bf16[512]{0:T(512)(128)(2,1)S(1)}, bf16[512]{0:T(512)(128)(2,1)}, u32[]{:S(2)}) copy-start(bf16[512]{0:T(512)(128)(2,1)} %param.28) | copy-start | bytes 3076
  284.2 83.4 %copy-start.15 = (bf16[64]{0:T(256)(128)(2,1)S(1)}, bf16[64]{0:T(256)(128)(2,1)}, u32[]{:S(2)}) copy-start(bf16[64]{0:T(256)(128)(2,1)} %param.30) | copy-start | bytes 388
  284.2 83.4 %copy-start.8 = (s32[512]{0:T(512)S(1)}, s32[512]{0:T(512)}, u32[]{:S(2)}) copy-start(s32[512]{0:T(512)} %param.33) | copy-start | bytes 6148
  285.6 476.2 %all-reduce.8.cloned.1.call-start = ((), (), s32[]{:S(2)}) async-start(), calls=%async_computation.1 | async-start | bytes 131072 | tf_op jit(solution)/shard_map/psum | solution.py:157
  285.7 86.3 %copy-start.12 = (bf16[512]{0:T(512)(128)(2,1)S(1)}, bf16[512]{0:T(512)(128)(2,1)}, u32[]{:S(2)}) copy-start(bf16[512]{0:T(512)(128)(2,1)} %param.32) | copy-start | bytes 3076
  285.7 86.3 %copy-start.13 = (u32[512]{0:T(512)S(1)}, u32[512]{0:T(512)}, u32[]{:S(2)}) copy-start(u32[512]{0:T(512)} %constant.157) | copy-start | bytes 6148
  367.7 345.7 %copy-start.14 = (bf16[64,512]{1,0:T(8,128)(2,1)S(1)}, bf16[64,512]{1,0:T(8,128)(2,1)}, u32[]{:S(2)}) copy-start(bf16[64,512]{1,0:T(8,128)(2,1)} %param.29) | copy-start | bytes 196612
  375.3 389.2 %copy-start.2 = (bf16[64,512]{1,0:T(8,128)(2,1)S(1)}, bf16[64,512]{1,0:T(8,128)(2,1)}, u32[]{:S(2)}) copy-start(bf16[64,512]{1,0:T(8,128)(2,1)} %param.31) | copy-start | bytes 196612
  714.4 388.5 %all-reduce.10.cloned.1.call-start = ((), (), s32[]{:S(2)}) async-start(), calls=%async_computation.3 | async-start | bytes 2097152
Sparse Core Ops, SparseCore 0:
  285.7 24.5 reduce-scatter.3
  714.5 47.1 all-reduce.7
  766.0 336.8 all-reduce.9
where the time goes:
time: 1110 us
  blocking collectives  679 us (61%)
  waiting for transfers between devices  384 us (35%)
  local copies, waits for them, and re-layouts  17.8 us (2%)
  between operations  14.8 us (1%)
    unnamed x5, waiting for transfers between devices  336 us
    unnamed x1, blocking collectives  248 us
    all_gather x1, blocking collectives, per_device(): lax.all_gather(query, 'req', axis=0, tiled=True)  91.2 us
    all_gather x1, blocking collectives, per_device(): lax.all_gather(key_new, 'req', axis=0, tiled=True)  87.8 us
    all_gather x1, blocking collectives, per_device(): lax.all_gather(resid, 'req', axis=0, tiled=True)  81.7 us
    all_gather x1, blocking collectives, per_device(): lax.all_gather(value_new, 'req', axis=0, tiled=True)  81.1 us
    all_gather x1, blocking collectives, per_device(): stream_all = lax.all_gather(stream_own, 'req', axis=0, tiled=True)  80.9 us
    psum x1, waiting for transfers between devices, per_device(): lax.psum(partial_value.astype(jnp.bfloat16), 'tp').astype(jnp.float32)  47.3 us
  transfers between devices with their start and end apart: 3, of which 2 were waited for; matrix products, arithmetic and copies ran while one was open for 1% of the time, Pallas kernels for 0%

commit v1 on v0

v1 whole, which is shorter than its diff:
```python
import functools
import math

import jax
import jax.numpy as jnp
from jax import lax
from jax.experimental import pallas as pl
from jax.experimental.pallas import tpu as pltpu
from jax.sharding import PartitionSpec as P

HD = 128
EPS = 1e-05
F32 = jnp.float32
BF16 = jnp.bfloat16
NEG = -1e30


def layer_kernel(
    dims,
    meta_ref,
    table_ref,
    vec_ref,
    q_ref,
    k_ref,
    v_ref,
    res_ref,
    kv_hbm,
    ow_hbm,
    up_hbm,
    dw_hbm,
    out_ref,
    kv,
    ow,
    up,
    rhs,
    g0,
    g1,
    p0,
    r0,
    p1,
    r1,
    a0,
    a1,
    part,
    stream,
    nbuf,
    x32,
    xbuf,
    hbuf,
    onehot,
    place,
    lhs,
    fsend,
    frecv,
    ysend,
    yrecv,
    zsend,
    zrecv,
    local_sem,
    zq_s,
    zq_r,
    zv_s,
    zv_r,
    pq_s,
    pq_r,
    pv_s,
    pv_r,
    pt_s,
    pt_r,
    ng_s,
    ng_r,
    yg_s,
    yg_r,
    cg_s,
    cg_r,
    hd_s,
    hd_r,
    fc_s,
    fc_r,
    fy_s,
    fy_r,
    fz_s,
    fz_r,
):
    Z, Y, C, T, W, K = dims
    PL = Y * C
    R = Z * PL * K
    H = W // HD
    D = W * T
    ZK = Z * K
    FL = up.shape[0]
    me = lax.axis_index("req")
    t = lax.axis_index("tp")
    core = lax.rem(me, C)
    y = lax.rem(me // C, Y)
    z = me // PL
    pid = lax.rem(me, PL)

    def z_peer(d):
        other = lax.rem(z + d, Z)
        return other, {"req": other * PL + pid}

    def plane_peer(d):
        other = lax.rem(pid + d, PL)
        return other, {"req": z * PL + other}

    def y_peer(d):
        other = lax.rem(y + d, Y)
        return other, {"req": z * PL + other * C + core}

    def tp_peer(d):
        other = lax.rem(t + d, T)
        return other, {"tp": other}

    core_peer = {"req": z * PL + y * C + (1 - core)}

    def send(src, dst, ssem, rsem, device):
        copy = pltpu.make_async_remote_copy(
            src_ref=src,
            dst_ref=dst,
            send_sem=ssem,
            recv_sem=rsem,
            device_id=device,
            device_id_type=pl.DeviceIdType.MESH,
        )
        copy.start()

    def drain(ref, sem):
        pltpu.make_async_copy(ref, ref, sem).wait()

    def each(count, body):
        def step(d, carry):
            body(d)
            return carry

        lax.fori_loop(1, count, step, 0)

    barrier = pltpu.get_barrier_semaphore()

    def greet(peer):
        def body(d):
            pl.semaphore_signal(
                barrier, inc=1, device_id=peer(d)[1], device_id_type=pl.DeviceIdType.MESH
            )

        return body

    each(Z, greet(z_peer))
    each(PL, greet(plane_peer))
    each(T, greet(tp_peer))

    loads = [
        pltpu.make_async_copy(kv_hbm, kv, local_sem.at[0]),
        pltpu.make_async_copy(ow_hbm, ow, local_sem.at[1]),
        pltpu.make_async_copy(up_hbm, up, local_sem.at[2]),
        pltpu.make_async_copy(dw_hbm, rhs.at[pl.ds(0, FL)], local_sem.at[3]),
    ]
    for load in loads:
        load.start()

    scale = 1.0 / math.sqrt(HD)
    product = q_ref[...].astype(F32) * k_ref[...].astype(F32)
    lane = lax.broadcasted_iota(jnp.int32, (K, HD), 1)
    packed = jnp.zeros((K, HD), F32)
    for h in range(H):
        s = jnp.sum(product[:, h * HD : (h + 1) * HD], axis=1, keepdims=True) * scale
        high = s.astype(BF16).astype(F32)
        mid = (s - high).astype(BF16).astype(F32)
        low = (s - high - mid).astype(BF16).astype(F32)
        packed = jnp.where(lane == h, high, packed)
        packed = jnp.where(lane == H + h, mid, packed)
        packed = jnp.where(lane == 2 * H + h, low, packed)
    g0[z, :, 0:W] = q_ref[...]
    g0[z, :, W : W + HD] = packed.astype(BF16)
    g1[z, :, 0:W] = v_ref[...]
    g1[z, :, W : 2 * W] = res_ref[...]

    pl.semaphore_wait(barrier, (Z - 1) + (PL - 1) + (T - 1))

    each(Z, lambda d: send(g0.at[z], g0.at[z], zq_s, zq_r, z_peer(d)[1]))
    each(Z, lambda d: send(g1.at[z], g1.at[z], zv_s, zv_r, z_peer(d)[1]))

    len_row = meta_ref[0:1, :]
    owner_row = meta_ref[1:2, :]
    order_row = meta_ref[2:3, :]
    base_row = meta_ref[3:4, :]
    sub_i = lax.broadcasted_iota(jnp.int32, (R, R), 0)
    lane_i = lax.broadcasted_iota(jnp.int32, (R, R), 1)
    lane_f = lane_i.astype(F32)

    def column(row, index):
        return jnp.sum(jnp.where(lane_f == index, row, 0.0), axis=1, keepdims=True)

    iota_col = lax.broadcasted_iota(jnp.int32, (R, 1), 0)
    owner_col = column(owner_row, iota_col.astype(F32))
    earlier = jnp.where((owner_col == owner_row) & (sub_i < lane_i), 1.0, 0.0)
    rank_row = jnp.sum(earlier, axis=0, keepdims=True)

    kap = lax.broadcasted_iota(jnp.int32, (R, ZK), 1)
    kap_request = (kap // K) * (PL * K) + pid * K + kap % K
    pick = jnp.where(
        lax.broadcasted_iota(jnp.int32, (R, ZK), 0) == kap_request, 1.0, 0.0
    ).astype(BF16)
    sub8 = lax.broadcasted_iota(jnp.int32, (8, R), 0)
    pair = jnp.where(sub8 == 0, owner_row, jnp.where(sub8 == 1, rank_row, 0.0)).astype(BF16)
    picked = jnp.dot(pair, pick, preferred_element_type=F32)
    target = picked[0:1, :] * K + picked[1:2, :] - (z * (PL * K)).astype(F32)
    sort = jnp.where(
        lax.broadcasted_iota(jnp.int32, (PL * K, ZK), 0).astype(F32) == target, 1.0, 0.0
    ).astype(BF16)

    def to_plane(source, flat, sendbuf, recvbuf, zs, zr, ps, pr):
        drain(source.at[pl.ds(0, Z - 1)], zr)
        for s in range(Z):
            flat[s * K : (s + 1) * K, :] = source[s].astype(F32)
        rows = jnp.dot(sort, flat[...].astype(BF16), preferred_element_type=F32)
        for d in range(PL):
            sendbuf[d] = rows[d * K : (d + 1) * K, :].astype(BF16)
        recvbuf[pid] = sendbuf[pid]

        def body(d):
            other, device = plane_peer(d)
            send(sendbuf.at[other], recvbuf.at[pid], ps, pr, device)

        each(PL, body)
        drain(source.at[pl.ds(0, Z - 1)], zs)

    def from_plane(recvbuf, pr):
        drain(recvbuf.at[pl.ds(0, PL - 1)], pr)
        total = recvbuf[0].astype(F32)
        for s in range(1, PL):
            total = total + recvbuf[s].astype(F32)
        return total

    to_plane(g0, a0, p0, r0, zq_s, zq_r, pq_s, pq_r)

    mine = (owner_row == me.astype(F32)) & (
        rank_row == lax.broadcasted_iota(jnp.int32, (8, R), 0).astype(F32)
    )
    mine_f = jnp.where(mine, 1.0, 0.0)
    own_len = jnp.sum(mine_f * len_row, axis=1, keepdims=True)[0:K]
    own_table = jnp.dot(
        mine_f.astype(BF16), table_ref[...].astype(F32).astype(BF16), preferred_element_type=F32
    )[0:K]
    tokens = kv.shape[1]
    page_len = 32
    token = lax.broadcasted_iota(jnp.int32, (1, tokens), 1)
    page = (token // page_len).astype(F32)
    offset = (token % page_len).astype(F32)
    len_hk = jnp.concatenate([own_len] * H, axis=0)
    table_hk = jnp.concatenate([own_table] * H, axis=0)
    valid = jnp.zeros((H * K, tokens), F32)
    for j in range(table_ref.shape[1]):
        hit = (table_hk[:, j : j + 1] == page) & (offset + float(j * page_len) < len_hk)
        valid = jnp.where(hit, 1.0, valid)
    valid = valid > 0.5

    to_plane(g1, a1, p1, r1, zv_s, zv_r, pv_s, pv_r)

    own0 = from_plane(r0, pq_r)
    q_own = own0[:, 0:W]
    head_of_row = lax.broadcasted_iota(jnp.int32, (H * K, W), 0) // K
    head_of_lane = lax.broadcasted_iota(jnp.int32, (H * K, W), 1) // HD
    q_block = jnp.where(
        head_of_row == head_of_lane, jnp.concatenate([q_own] * H, axis=0), 0.0
    ).astype(BF16)
    self_col = jnp.concatenate(
        [
            own0[:, W + h : W + h + 1]
            + own0[:, W + H + h : W + H + h + 1]
            + own0[:, W + 2 * H + h : W + 2 * H + h + 1]
            for h in range(H)
        ],
        axis=0,
    )
    loads[0].wait()
    scores = (
        lax.dot_general(q_block, kv[0], (((1,), (1,)), ((), ())), preferred_element_type=F32)
        * scale
    )
    scores = jnp.where(valid, scores, NEG)
    top = jnp.maximum(jnp.max(scores, axis=1, keepdims=True), self_col)
    weights = jnp.where(valid, jnp.exp(scores - top), 0.0)
    self_weight = jnp.exp(self_col - top)
    total = jnp.sum(weights, axis=1, keepdims=True) + self_weight
    wide = jnp.dot(weights.astype(BF16), kv[1], preferred_element_type=F32)
    wide = jnp.where(head_of_row == head_of_lane, wide, 0.0)
    numer = wide[:, 0:HD]
    for h in range(1, H):
        numer = numer + wide[:, h * HD : (h + 1) * HD]

    own1 = from_plane(r1, pv_r)
    v_fold = jnp.concatenate([own1[:, h * HD : (h + 1) * HD] for h in range(H)], axis=0)
    numer = numer + self_weight.astype(BF16).astype(F32) * v_fold
    attn_fold = numer / total
    attn = jnp.concatenate([attn_fold[h * K : (h + 1) * K, :] for h in range(H)], axis=1).astype(
        BF16
    )

    loads[1].wait()
    part[t] = jnp.dot(attn, ow[...], preferred_element_type=F32)
    here = pl.ds(pl.multiple_of(t * W, W), W)
    part[t, :, here] = part[t, :, here] + (own1[:, W : 2 * W] + vec_ref[0:1, :])
    each(T, lambda d: send(part.at[t], part.at[t], pt_s, pt_r, tp_peer(d)[1]))
    drain(part.at[pl.ds(0, T - 1)], pt_r)
    summed = part[0]
    for s in range(1, T):
        summed = summed + part[s]
    rows_f = summed.astype(BF16).astype(F32)
    mean = jnp.sum(rows_f, axis=1, keepdims=True) * (1.0 / D)
    centred = rows_f - mean
    var = jnp.sum(centred * centred, axis=1, keepdims=True) * (1.0 / D)
    inverse = lax.rsqrt(var + EPS)
    stream[...] = rows_f
    mine_f32 = stream[:, here]
    nbuf[z] = ((mine_f32 - mean) * inverse * vec_ref[1:2, :] + vec_ref[2:3, :]).astype(BF16)

    each(Z, lambda d: send(nbuf.at[z], nbuf.at[z], ng_s, ng_r, z_peer(d)[1]))

    place_i = lax.broadcasted_iota(jnp.int32, (R, 1), 0)
    place_k = place_i % K
    place_z = (place_i // K) % Z
    place_y = (place_i // ZK) % Y
    place_c = place_i // (ZK * Y)
    natural = ((place_z * Y + place_y) * C + place_c) * K + place_k
    request = column(order_row, natural.astype(F32))
    slot = column(base_row + rank_row, request)
    onehot[...] = jnp.where(lane_f == slot, 1.0, 0.0).astype(BF16)
    my_base = (core * (Y * ZK) + y * ZK + z * K).astype(F32)
    lane_p = lax.broadcasted_iota(jnp.int32, (R, 2 * FL), 1)
    place[...] = jnp.where(
        (slot == my_base + (lane_p - FL).astype(F32)) & (lane_p >= FL) & (lane_p < FL + K),
        1.0,
        0.0,
    )
    rhs[FL : 2 * FL, :] = jnp.concatenate(
        [mine_f32, jnp.zeros((FL - K, W), F32)], axis=0
    ).astype(BF16)
    drain(p0.at[pl.ds(0, PL - 1)], pq_s)
    drain(p1.at[pl.ds(0, PL - 1)], pv_s)
    drain(part.at[pl.ds(0, T - 1)], pt_s)

    drain(nbuf.at[pl.ds(0, Z - 1)], ng_r)
    for s in range(Z):
        x32[s * K : (s + 1) * K, :] = nbuf[s].astype(F32)
    xbuf[core, y] = x32[...].astype(BF16)
    for d in range(1, Y):
        other, device = y_peer(d)
        send(xbuf.at[core, y], xbuf.at[core, y], yg_s.at[d], yg_r.at[y], device)
    send(xbuf.at[core, y], xbuf.at[core, y], cg_s.at[0], cg_r.at[y], core_peer)
    for d in range(1, Y):
        other, device = y_peer(d)
        drain(xbuf.at[core, other], yg_r.at[other])
        send(xbuf.at[core, other], xbuf.at[core, other], cg_s.at[d], cg_r.at[other], core_peer)
    for s in range(Y):
        drain(xbuf.at[1 - core, s], cg_r.at[s])

    loads[2].wait()
    hidden = lax.dot_general(
        up[...], xbuf[...].reshape(R, W), (((1,), (1,)), ((), ())), preferred_element_type=F32
    )
    hbuf[t] = hidden.astype(BF16)
    each(T, lambda d: send(hbuf.at[t], hbuf.at[t], hd_s, hd_r, tp_peer(d)[1]))
    up_bias = jnp.sum(
        jnp.where(
            lax.broadcasted_iota(jnp.int32, (FL, FL), 0)
            == lax.broadcasted_iota(jnp.int32, (FL, FL), 1),
            vec_ref[4:5, 0:FL],
            0.0,
        ),
        axis=1,
        keepdims=True,
    )
    drain(nbuf.at[pl.ds(0, Z - 1)], ng_s)
    for d in range(1, Y):
        drain(xbuf.at[core, y], yg_s.at[d])
    for d in range(Y):
        drain(xbuf.at[core, y], cg_s.at[d])
    drain(hbuf.at[pl.ds(0, T - 1)], hd_r)
    before = hbuf[0].astype(F32)
    for s in range(1, T):
        before = before + hbuf[s].astype(F32)
    before = before + up_bias
    active = 0.5 * before * (1.0 + lax.erf(before * math.sqrt(0.5)))
    active = jnp.concatenate([active, jnp.zeros((FL, R), F32)], axis=0).astype(BF16)
    lhs[...] = (
        lax.dot_general(onehot[...], active, (((1,), (1,)), ((), ())), preferred_element_type=F32)
        + place[...]
    ).astype(BF16)
    loads[3].wait()

    def feed_rows(half, block):
        start = pl.multiple_of(half * (Y * ZK) + block * ZK, ZK)
        return jnp.dot(lhs[pl.ds(start, ZK), :], rhs[...], preferred_element_type=F32)

    for d in range(1, Y + 1):
        block = lax.rem(y + d, Y)
        fsend[block] = feed_rows(1 - core, block).astype(BF16)
        send(fsend.at[block], frecv.at[block], fc_s.at[block], fc_r.at[block], core_peer)
    for d in range(1, Y):
        block, device = y_peer(d)
        mine_half = feed_rows(core, block)
        drain(frecv.at[block], fc_r.at[block])
        ysend[block] = (mine_half + frecv[block].astype(F32)).astype(BF16)
        send(ysend.at[block], yrecv.at[y], fy_s.at[block], fy_r.at[y], device)
    mine_half = feed_rows(core, y)
    drain(frecv.at[y], fc_r.at[y])
    rows = mine_half + frecv[y].astype(F32)
    for d in range(1, Y):
        other, _ = y_peer(d)
        drain(yrecv.at[other], fy_r.at[other])
        rows = rows + yrecv[other].astype(F32)
    for s in range(Z):
        zsend[s] = rows[s * K : (s + 1) * K, :].astype(BF16)
    zrecv[z] = zsend[z]

    def scatter(d):
        other, device = z_peer(d)
        send(zsend.at[other], zrecv.at[z], fz_s, fz_r, device)

    each(Z, scatter)
    drain(hbuf.at[pl.ds(0, T - 1)], hd_s)
    for s in range(Y):
        drain(fsend.at[s], fc_s.at[s])
    for d in range(1, Y):
        other, _ = y_peer(d)
        drain(ysend.at[other], fy_s.at[other])
    drain(zrecv.at[pl.ds(0, Z - 1)], fz_r)
    final = zrecv[0].astype(F32)
    for s in range(1, Z):
        final = final + zrecv[s].astype(F32)
    out_ref[...] = (final + vec_ref[3:4, :]).astype(BF16)
    drain(zsend.at[pl.ds(0, Z - 1)], fz_s)


def chip_grid(devices):
    cores = 2
    along_y = 4 if devices >= 32 else 2
    return devices // (along_y * cores), along_y, cores


def per_device(
    query,
    key_new,
    value_new,
    resid,
    lengths,
    owner,
    page_table,
    kv_pool,
    out_weight,
    out_bias,
    norm_gain,
    norm_bias,
    up_weight_t,
    up_bias,
    down_weight,
    down_bias,
    order,
):
    K, W = query.shape
    devices = lax.axis_size("req")
    T = lax.axis_size("tp")
    Z, Y, C = chip_grid(devices)
    PL = Y * C
    R = devices * K
    D = W * T
    FL = up_weight_t.shape[0]
    pages, page_len = kv_pool.shape[1], kv_pool.shape[2]
    tokens = pages * page_len
    base = (owner % C) * (Y * Z * K) + ((owner // C) % Y) * (Z * K) + (owner // PL) * K
    meta = jnp.stack([lengths, owner, order, base]).astype(F32)
    vec = jnp.stack(
        [out_bias, norm_gain, norm_bias, down_bias, jnp.pad(up_bias, (0, W - FL))]
    ).astype(F32)
    vmem = pl.BlockSpec(memory_space=pltpu.VMEM)
    anywhere = pl.BlockSpec(memory_space=pl.ANY)
    dma = pltpu.SemaphoreType.DMA
    return pl.pallas_call(
        functools.partial(layer_kernel, (Z, Y, C, T, W, K)),
        out_shape=jax.ShapeDtypeStruct((K, W), BF16),
        in_specs=[vmem] * 7 + [anywhere] * 4,
        out_specs=vmem,
        scratch_shapes=[
            pltpu.VMEM((2, tokens, W), BF16),
            pltpu.VMEM((W, D), BF16),
            pltpu.VMEM((FL, W), BF16),
            pltpu.VMEM((2 * FL, W), BF16),
            pltpu.VMEM((Z, K, W + HD), BF16),
            pltpu.VMEM((Z, K, 2 * W), BF16),
            pltpu.VMEM((PL, K, W + HD), BF16),
            pltpu.VMEM((PL, K, W + HD), BF16),
            pltpu.VMEM((PL, K, 2 * W), BF16),
            pltpu.VMEM((PL, K, 2 * W), BF16),
            pltpu.VMEM((Z * K, W + HD), F32),
            pltpu.VMEM((Z * K, 2 * W), F32),
            pltpu.VMEM((T, K, D), F32),
            pltpu.VMEM((K, D), F32),
            pltpu.VMEM((Z, K, W), BF16),
            pltpu.VMEM((Z * K, W), F32),
            pltpu.VMEM((C, Y, Z * K, W), BF16),
            pltpu.VMEM((T, FL, R), BF16),
            pltpu.VMEM((R, R), BF16),
            pltpu.VMEM((R, 2 * FL), F32),
            pltpu.VMEM((R, 2 * FL), BF16),
            pltpu.VMEM((Y, Z * K, W), BF16),
            pltpu.VMEM((Y, Z * K, W), BF16),
            pltpu.VMEM((Y, Z * K, W), BF16),
            pltpu.VMEM((Y, Z * K, W), BF16),
            pltpu.VMEM((Z, K, W), BF16),
            pltpu.VMEM((Z, K, W), BF16),
            dma((4,)),
        ]
        + [dma(())] * 12
        + [dma((Y,))] * 4
        + [dma(())] * 2
        + [dma((Y,))] * 4
        + [dma(())] * 2,
        compiler_params=pltpu.CompilerParams(
            collective_id=0, has_side_effects=True, vmem_limit_bytes=48 * 1024 * 1024
        ),
    )(
        meta,
        page_table,
        vec,
        query,
        key_new,
        value_new,
        resid,
        kv_pool.reshape(2, tokens, W),
        out_weight,
        up_weight_t,
        down_weight,
    )


def solution(mesh):
    in_specs = (
        P("req", "tp"),
        P("req", "tp"),
        P("req", "tp"),
        P("req", "tp"),
        P(),
        P(),
        P(),
        P(None, "req", None, "tp"),
        P("tp", None),
        P("tp"),
        P("tp"),
        P("tp"),
        P("req", "tp"),
        P("req"),
        P("req", "tp"),
        P("tp"),
        P(),
    )
    return jax.shard_map(
        per_device, mesh=mesh, in_specs=in_specs, out_specs=P("req", "tp"), check_vma=False
    )
```

time: 1110 us -> 84.9 us (0.08)
  blocking collectives: 679 us -> 0 us
  waiting for transfers between devices: 384 us -> 0 us
  Pallas kernels: 0 us -> 70.6 us
  between operations: 14.8 us -> 0.05 us
    all_gather x5 -> x0, blocking collectives: 423 us -> none  [the longest x1 91.2 us: per_device(): lax.all_gather(query, 'req', axis=0, tiled=True)]
    unnamed x5 -> x0, waiting for transfers between devices: 336 us -> none
    unnamed x1 -> x0, blocking collectives: 248 us -> none
    pallas_call x0 -> x1, Pallas kernels: none -> 70.6 us  [per_device(): pl.pallas_call(functools.partial(layer_kernel, (Z, Y, C, T, W, K)), out_s...]
    psum x1 -> x0, waiting for transfers between devices: 47.3 us -> none  [per_device(): lax.psum(partial_value.astype(jnp.bfloat16), 'tp').astype(jnp.float32)]
  transfers between devices with their start and end apart: 3 -> 0, of which waited for: 2 -> 0; matrix products, arithmetic and copies ran while one was open for 1% -> 0% of each run, Pallas kernels for 0% -> 0%
where the time goes in v1:
time: 84.9 us; the launch traced here: 84.3 us
  Pallas kernels  70.6 us (83%)
  local copies, waits for them, and re-layouts  12.3 us (14%)
  other arithmetic  1.44 us (2%)
    pallas_call x1, Pallas kernels, per_device(): pl.pallas_call(functools.partial(layer_kernel, (Z, Y, C, T, W, K)), out_s...  70.6 us
    unnamed x18, local copies, waits for them, and re-layouts  8.85 us
    another operation x6, local copies, waits for them, and re-layouts, per_device(): jnp.stack([out_bias, norm_gain, norm_bias, down_bias, jnp.pad(up_bias, (0...  2.77 us

profile of v1, /device:TPU:1, one launch (start us, length us, event | category | flops | bytes accessed | tf_op | source)
XLA Modules:
  0.0 84.3 jit_solution(9002821982832326090)
XLA Ops:
  0.0 0.7 pad.4
  0.7 0.7 stack.38
  1.4 0.7 stack.39
  2.0 0.7 stack.40
  2.7 0.7 stack.41
  3.4 0.7 fusion.2
  4.1 0.7 add_convert_fusion.meta_ref
  4.9 0.9 %copy.18.table_ref = s32[512,16]{1,0:T(8,128)S(1)} copy(s32[512,16]{0,1:T(8,128)} %param.23) | data formatting | bytes 65536 | tf_op args[6]
  5.8 0.0 copy-start
  5.8 1.6 %copy-done = bf16[512,2048]{1,0:T(8,128)(2,1)S(1)} copy-done((bf16[512,2048]{1,0:T(8,128)(2,1)S(1)}, bf16[512,2048]{1,0:T(8,128)(2,1)}, u32[]{:S(2)}) %copy-start) | copy-done | bytes 2097176
  7.4 0.0 copy-start.1
  7.4 1.4 %copy-done.1 = bf16[2,22,32,512]{3,2,1,0:T(8,128)(2,1)S(1)} copy-done((bf16[2,22,32,512]{3,2,1,0:T(8,128)(2,1)S(1)}, bf16[2,22,32,512]{3,2,1,0:T(8,128)(2,1)}, u32[]{:S(2)}) %copy-start.1) | copy-done | bytes 1441816
  8.7 0.0 copy-start.2
  8.7 0.8 copy-done.2
  9.6 0.0 copy-start.3
  9.6 0.8 copy-done.3
  10.4 0.0 copy-start.4
  10.4 0.7 copy-done.4
  11.1 0.0 copy-start.5
  11.1 0.7 copy-done.5
  11.8 0.7 copy-done.6
  12.5 0.7 copy-done.7
  13.2 70.6 %shard_map.163 = bf16[4,512]{1,0:T(4,128)(2,1)S(1)} custom-call(f32[4,512]{1,0:T(4,128)S(1)} %add_convert_fusion.meta_ref, s32[512,16]{1,0:T(8,128)S(1)} %copy.18.table_ref, f32[5,512]{1,0:T(8,128)S(1)} %convert_element_type.9.vec_ref, bf16[4,512]{1,0:T(4,128)(2,1)S(1)} %copy-done.4, bf16[4,512]{1,0:T(4,128)(2,1)S(1)} %copy-done.5, ...), custom_call_target="tpu_custom_call" | custom-call | tf_op jit(solution)/shard_map/pallas_call | solution.py:479
  83.7 0.6 copy.20
  (5 shorter events, 0.0 us)
Async XLA Ops:
  5.8 1.6 %copy-start = (bf16[512,2048]{1,0:T(8,128)(2,1)S(1)}, bf16[512,2048]{1,0:T(8,128)(2,1)}, u32[]{:S(2)}) copy-start(bf16[512,2048]{1,0:T(8,128)(2,1)} %ow_hbm.1) | copy-start | bytes 6291460
  7.4 1.4 %copy-start.1 = (bf16[2,22,32,512]{3,2,1,0:T(8,128)(2,1)S(1)}, bf16[2,22,32,512]{3,2,1,0:T(8,128)(2,1)}, u32[]{:S(2)}) copy-start(bf16[2,22,32,512]{3,2,1,0:T(8,128)(2,1)} %param.24) | copy-start | bytes 4325380
  8.7 0.8 copy-start.2
  9.6 0.8 copy-start.3
  10.4 0.7 copy-start.4
  11.1 0.7 copy-start.5
  11.8 0.7 copy-start.6
  12.5 0.7 copy-start.7

commit v2 on v1

v2 whole, which is shorter than its diff:
```python
import functools
import math

import jax
import jax.numpy as jnp
from jax import lax
from jax.experimental import pallas as pl
from jax.experimental.pallas import tpu as pltpu
from jax.sharding import PartitionSpec as P

HD = 128
EPS = 1e-05
F32 = jnp.float32
BF16 = jnp.bfloat16
NEG = -1e30


def over(x, n):
    return lax.shift_right_logical(x, n.bit_length() - 1)


def within(x, n):
    return x & (n - 1)


def iota(shape, dim):
    return lax.broadcasted_iota(jnp.int32, shape, dim)


def hot(mask):
    return jnp.where(mask, 1.0, 0.0).astype(BF16)


def layer_kernel(
    dims,
    q_hbm,
    k_hbm,
    v_hbm,
    res_hbm,
    owner_hbm,
    order_hbm,
    len_hbm,
    table_hbm,
    kv_hbm,
    ow_hbm,
    up_hbm,
    dw_hbm,
    ob_hbm,
    ng_hbm,
    nb_hbm,
    ub_hbm,
    db_hbm,
    out_ref,
    q_ref,
    k_ref,
    meta_ref,
    table_ref,
    ob_ref,
    ng_ref,
    nb_ref,
    ub_ref,
    db_ref,
    kv,
    ow,
    wts,
    g0,
    g1,
    p0,
    r0,
    p1,
    r1,
    a0,
    a1,
    part,
    stream,
    nbuf,
    x32,
    hbuf,
    abuf,
    zsend,
    zrecv,
    local_sem,
    zq_s,
    zq_r,
    zv_s,
    zv_r,
    pq_s,
    pq_r,
    pv_s,
    pv_r,
    pt_s,
    pt_r,
    ng_s,
    ng_r,
    hd_s,
    hd_r,
    wy_s,
    wy_r,
    wc_s,
    wc_r,
    ay_s,
    ay_r,
    ac_s,
    ac_r,
    fz_s,
    fz_r,
):
    Z, Y, C, T, W, K = dims
    PL = Y * C
    R = Z * PL * K
    H = W // HD
    D = W * T
    ZK = Z * K
    FL = up_hbm.shape[0]
    BLK = ZK + 8
    me = lax.axis_index("req")
    t = lax.axis_index("tp")
    core = lax.rem(me, C)
    y = lax.rem(me // C, Y)
    z = me // PL
    pid = lax.rem(me, PL)

    def far_first(i, n):
        return n // 2 + (i // 2) * (1 - 2 * (i % 2))

    def z_peer(i):
        other = lax.rem(z + far_first(i, Z), Z)
        return other, {"req": other * PL + pid}

    plane_steps = sorted(
        [(a, b) for a in range(Y) for b in range(C) if a or b],
        key=lambda step: -min(step[0], Y - step[0]),
    )

    def plane_peer(step):
        other = lax.rem(y + step[0], Y) * C + lax.rem(core + step[1], C)
        return other, {"req": z * PL + other}

    def y_peer(i):
        other = lax.rem(y + far_first(i, Y), Y)
        return other, {"req": z * PL + other * C + core}

    def tp_peer(i):
        other = lax.rem(t + far_first(i, T), T)
        return other, {"tp": other}

    core_peer = {"req": z * PL + y * C + (1 - core)}

    def send(src, dst, ssem, rsem, device):
        copy = pltpu.make_async_remote_copy(
            src_ref=src,
            dst_ref=dst,
            send_sem=ssem,
            recv_sem=rsem,
            device_id=device,
            device_id_type=pl.DeviceIdType.MESH,
        )
        copy.start()

    def drain(ref, sem):
        pltpu.make_async_copy(ref, ref, sem).wait()

    def each(count, body):
        def step(d, carry):
            body(d)
            return carry

        lax.fori_loop(1, count, step, 0)

    pairs = [
        (q_hbm, q_ref),
        (k_hbm, k_ref),
        (q_hbm, g0.at[z, :, pl.ds(0, W)]),
        (v_hbm, g1.at[z, :, pl.ds(0, W)]),
        (res_hbm, g1.at[z, :, pl.ds(W, W)]),
        (owner_hbm, meta_ref.at[0]),
        (order_hbm, meta_ref.at[1]),
        (len_hbm, meta_ref.at[2]),
        (table_hbm, table_ref),
        (kv_hbm, kv),
        (ow_hbm, ow),
        (up_hbm, wts.at[pid, pl.ds(0, FL)]),
        (dw_hbm, wts.at[pid, pl.ds(FL, FL)]),
        (ob_hbm, ob_ref),
        (ng_hbm, ng_ref),
        (nb_hbm, nb_ref),
        (ub_hbm, ub_ref),
        (db_hbm, db_ref),
    ]
    loads = [pltpu.make_async_copy(a, b, local_sem.at[i]) for i, (a, b) in enumerate(pairs)]

    def vector(ref):
        return ref[...].astype(F32).reshape(1, ref.shape[0])

    barrier = pltpu.get_barrier_semaphore()

    def greet(peer):
        def body(d):
            pl.semaphore_signal(
                barrier, inc=1, device_id=peer(d)[1], device_id_type=pl.DeviceIdType.MESH
            )

        return body

    each(Z, greet(z_peer))
    for step in plane_steps:
        greet(plane_peer)(step)
    each(T, greet(tp_peer))

    for load in loads:
        load.start()

    scale = 1.0 / math.sqrt(HD)
    loads[0].wait()
    loads[1].wait()
    product = q_ref[...].astype(F32) * k_ref[...].astype(F32)
    lane = lax.broadcasted_iota(jnp.int32, (K, HD), 1)
    packed = jnp.zeros((K, HD), F32)
    for h in range(H):
        s = jnp.sum(product[:, h * HD : (h + 1) * HD], axis=1, keepdims=True) * scale
        high = s.astype(BF16).astype(F32)
        mid = (s - high).astype(BF16).astype(F32)
        low = (s - high - mid).astype(BF16).astype(F32)
        packed = jnp.where(lane == h, high, packed)
        packed = jnp.where(lane == H + h, mid, packed)
        packed = jnp.where(lane == 2 * H + h, low, packed)
    g0[z, :, W : W + HD] = packed.astype(BF16)

    for load in loads[2:5]:
        load.wait()
    pl.semaphore_wait(barrier, (Z - 1) + (PL - 1) + (T - 1))

    each(Z, lambda d: send(g0.at[z], g0.at[z], zq_s, zq_r, z_peer(d)[1]))
    each(Z, lambda d: send(g1.at[z], g1.at[z], zv_s, zv_r, z_peer(d)[1]))

    for load in [loads[11], loads[12], loads[16]]:
        load.wait()
    spread = hot(iota((FL, W), 1) == pid * FL + iota((FL, W), 0))
    bias8 = jnp.where(iota((8, FL), 0) == 0, vector(ub_ref), 0.0)
    wts[pid, 2 * FL : 2 * FL + 8, :] = jnp.dot(
        bias8.astype(BF16), spread, preferred_element_type=F32
    ).astype(BF16)
    for i in range(1, Y):
        send(wts.at[pid], wts.at[pid], wy_s.at[i], wy_r.at[y], y_peer(i)[1])
    send(wts.at[pid], wts.at[pid], wc_s.at[0], wc_r.at[y], core_peer)

    for load in loads[5:9]:
        load.wait()
    owner_i = meta_ref[0]
    owner_row = owner_i.astype(F32)
    order_i = meta_ref[1]
    len_row = meta_ref[2].astype(F32)

    owners = Z * PL
    lanes = min(R, HD)
    earlier = hot(iota((lanes, lanes), 0) < iota((lanes, lanes), 1))
    ones = jnp.ones((lanes, lanes), BF16)
    before = None
    ranks = []
    for b in range(R // lanes):
        mask = iota((owners, lanes), 0) == owner_i[:, b * lanes : (b + 1) * lanes]
        mask_f = jnp.where(mask, 1.0, 0.0)
        count = jnp.dot(mask_f.astype(BF16), earlier, preferred_element_type=F32)
        if before is not None:
            count = count + jnp.dot(before.astype(BF16), ones, preferred_element_type=F32)
        ranks.append(jnp.sum(mask_f * count, axis=0, keepdims=True))
        before = mask_f if before is None else before + mask_f
    rank_row = jnp.concatenate(ranks, axis=1)

    KL = max(ZK, HD)
    kap = iota((1, KL), 1)
    kap_request = over(kap, K) * (PL * K) + pid * K + within(kap, K)
    pick = hot(iota((R, KL), 0) == kap_request)
    sub8 = iota((8, R), 0)

    def stacked(*rows):
        total = jnp.zeros((8, R), F32)
        for i, row in enumerate(rows):
            total = jnp.where(sub8 == i, row.astype(F32), total)
        return total.astype(BF16)

    picked = jnp.dot(
        stacked(owner_row, rank_row, over(order_i, 16), within(order_i, 16)),
        pick,
        preferred_element_type=F32,
    )
    target = picked[0:1, 0:ZK] * K + picked[1:2, 0:ZK] - (z * (PL * K)).astype(F32)
    sort = hot(iota((PL * K, ZK), 0).astype(F32) == target)
    out_request = (picked[2:3, :] * 16.0 + picked[3:4, :]).astype(jnp.int32)

    def to_plane(source, flat, sendbuf, recvbuf, zs, zr, ps, pr):
        drain(source.at[pl.ds(0, Z - 1)], zr)
        for s in range(Z):
            flat[s * K : (s + 1) * K, :] = source[s].astype(F32)
        rows = jnp.dot(sort, flat[...].astype(BF16), preferred_element_type=F32)
        for d in range(PL):
            sendbuf[d] = rows[d * K : (d + 1) * K, :].astype(BF16)
        recvbuf[pid] = sendbuf[pid]

        def body(step):
            other, device = plane_peer(step)
            send(sendbuf.at[other], recvbuf.at[pid], ps, pr, device)

        for step in plane_steps:
            body(step)
        drain(source.at[pl.ds(0, Z - 1)], zs)

    def from_plane(recvbuf, pr):
        drain(recvbuf.at[pl.ds(0, PL - 1)], pr)
        total = recvbuf[0].astype(F32)
        for s in range(1, PL):
            total = total + recvbuf[s].astype(F32)
        return total

    to_plane(g0, a0, p0, r0, zq_s, zq_r, pq_s, pq_r)
    for i in range(1, Y):
        other, _ = y_peer(i)
        arrived = wts.at[other * C + core]
        drain(arrived, wy_r.at[other])
        send(arrived, arrived, wc_s.at[i], wc_r.at[other], core_peer)

    mine = (owner_row == me.astype(F32)) & (
        rank_row == sub8.astype(F32)
    )
    mine_f = jnp.where(mine, 1.0, 0.0)
    own_len = jnp.sum(mine_f * len_row, axis=1, keepdims=True)[0:K]
    own_table = lax.dot_general(
        mine_f.astype(BF16),
        table_ref[...].astype(F32).astype(BF16),
        (((1,), (1,)), ((), ())),
        preferred_element_type=F32,
    )[0:K]
    tokens = kv.shape[1]
    page_len = 32
    token = lax.broadcasted_iota(jnp.int32, (1, tokens), 1)
    page = over(token, page_len).astype(F32)
    offset = within(token, page_len).astype(F32)
    len_hk = jnp.concatenate([own_len] * H, axis=0)
    table_hk = jnp.concatenate([own_table] * H, axis=0)
    valid = jnp.zeros((H * K, tokens), F32)
    for j in range(table_ref.shape[0]):
        hit = (table_hk[:, j : j + 1] == page) & (offset + float(j * page_len) < len_hk)
        valid = jnp.where(hit, 1.0, valid)
    valid = valid > 0.5

    to_plane(g1, a1, p1, r1, zv_s, zv_r, pv_s, pv_r)

    own0 = from_plane(r0, pq_r)
    q_own = own0[:, 0:W]
    head_of_row = over(iota((H * K, W), 0), K)
    head_of_lane = over(iota((H * K, W), 1), HD)
    q_block = jnp.where(
        head_of_row == head_of_lane, jnp.concatenate([q_own] * H, axis=0), 0.0
    ).astype(BF16)
    self_col = jnp.concatenate(
        [
            own0[:, W + h : W + h + 1]
            + own0[:, W + H + h : W + H + h + 1]
            + own0[:, W + 2 * H + h : W + 2 * H + h + 1]
            for h in range(H)
        ],
        axis=0,
    )
    loads[9].wait()
    scores = (
        lax.dot_general(q_block, kv[0], (((1,), (1,)), ((), ())), preferred_element_type=F32)
        * scale
    )
    scores = jnp.where(valid, scores, NEG)
    top = jnp.maximum(jnp.max(scores, axis=1, keepdims=True), self_col)
    weights = jnp.where(valid, jnp.exp(scores - top), 0.0)
    self_weight = jnp.exp(self_col - top)
    total = jnp.sum(weights, axis=1, keepdims=True) + self_weight
    wide = jnp.dot(weights.astype(BF16), kv[1], preferred_element_type=F32)
    wide = jnp.where(head_of_row == head_of_lane, wide, 0.0)
    numer = wide[:, 0:HD]
    for h in range(1, H):
        numer = numer + wide[:, h * HD : (h + 1) * HD]

    own1 = from_plane(r1, pv_r)
    v_fold = jnp.concatenate([own1[:, h * HD : (h + 1) * HD] for h in range(H)], axis=0)
    numer = numer + self_weight.astype(BF16).astype(F32) * v_fold
    attn_fold = numer / total
    attn = jnp.concatenate([attn_fold[h * K : (h + 1) * K, :] for h in range(H)], axis=1).astype(
        BF16
    )

    loads[10].wait()
    for load in [loads[13], loads[14], loads[15], loads[17]]:
        load.wait()
    part[t] = jnp.dot(attn, ow[...], preferred_element_type=F32)
    here = pl.ds(pl.multiple_of(t * W, W), W)
    part[t, :, here] = part[t, :, here] + (own1[:, W : 2 * W] + vector(ob_ref))
    each(T, lambda d: send(part.at[t], part.at[t], pt_s, pt_r, tp_peer(d)[1]))
    drain(part.at[pl.ds(0, T - 1)], pt_r)
    summed = part[0]
    for s in range(1, T):
        summed = summed + part[s]
    rows_f = summed.astype(BF16).astype(F32)
    mean = jnp.sum(rows_f, axis=1, keepdims=True) * (1.0 / D)
    centred = rows_f - mean
    var = jnp.sum(centred * centred, axis=1, keepdims=True) * (1.0 / D)
    inverse = lax.rsqrt(var + EPS)
    stream[...] = rows_f
    mine_f32 = stream[:, here]
    nbuf[z] = ((mine_f32 - mean) * inverse * vector(ng_ref) + vector(nb_ref)).astype(BF16)

    each(Z, lambda d: send(nbuf.at[z], nbuf.at[z], ng_s, ng_r, z_peer(d)[1]))

    found = jnp.dot(
        stacked(owner_row, rank_row), hot(iota((R, KL), 0) == out_request), preferred_element_type=F32
    )
    home = found[0:1, :].astype(jnp.int32)
    block = (within(home, C) * Y + within(over(home, C), Y)) * BLK + found[1:2, :].astype(jnp.int32)
    row_at = block + over(home, PL) * K
    stream_at = jnp.where(over(home, PL) == z, block + ZK, -1)
    at8 = jnp.where(
        iota((8, KL), 0) == 0,
        row_at.astype(F32),
        stream_at.astype(F32),
    )
    at_col = jnp.transpose(at8)[0:ZK, :]
    lane_a = iota((ZK, PL * BLK), 1).astype(F32)
    choose = jnp.concatenate(
        [hot(lane_a == at_col[:, 0:1]), hot(lane_a == at_col[:, 1:2])], axis=0
    )
    abuf[core, y, ZK:BLK, :] = jnp.concatenate(
        [mine_f32, jnp.zeros((BLK - ZK - K, W), F32)], axis=0
    ).astype(BF16)
    drain(p0.at[pl.ds(0, PL - 1)], pq_s)
    drain(p1.at[pl.ds(0, PL - 1)], pv_s)
    drain(part.at[pl.ds(0, T - 1)], pt_s)

    drain(nbuf.at[pl.ds(0, Z - 1)], ng_r)
    for s in range(Z):
        x32[s * K : (s + 1) * K, :] = nbuf[s].astype(F32)
    for i in range(1, Y + 1):
        if i < Y:
            other, _ = y_peer(i)
            arrived = other * C + (1 - core)
        else:
            arrived = y * C + (1 - core)
            other = y
        drain(wts.at[arrived], wc_r.at[other])

    up = jnp.concatenate([wts[p, 0:FL, :] for p in range(PL)], axis=0)
    hidden = lax.dot_general(
        x32[...].astype(BF16), up, (((1,), (1,)), ((), ())), preferred_element_type=F32
    )
    hbuf[t] = hidden.astype(BF16)
    each(T, lambda d: send(hbuf.at[t], hbuf.at[t], hd_s, hd_r, tp_peer(d)[1]))
    up_bias = wts[0, 2 * FL : 2 * FL + 8, :].astype(F32)
    for p in range(1, PL):
        up_bias = up_bias + wts[p, 2 * FL : 2 * FL + 8, :].astype(F32)
    down = jnp.concatenate([wts[p, FL : 2 * FL, :] for p in range(PL)], axis=0)
    drain(nbuf.at[pl.ds(0, Z - 1)], ng_s)
    for i in range(1, Y):
        drain(wts.at[pid], wy_s.at[i])
    for i in range(Y):
        drain(wts.at[pid], wc_s.at[i])
    drain(hbuf.at[pl.ds(0, T - 1)], hd_r)
    before = hbuf[0].astype(F32)
    for s in range(1, T):
        before = before + hbuf[s].astype(F32)
    before = before + up_bias[0:1, 0 : PL * FL]
    active = 0.5 * before * (1.0 + lax.erf(before * math.sqrt(0.5)))
    abuf[core, y, 0:ZK, 0 : PL * FL] = active.astype(BF16)
    if PL * FL < W:
        abuf[core, y, 0:ZK, PL * FL : W] = jnp.zeros((ZK, W - PL * FL), BF16)

    for i in range(1, Y):
        send(abuf.at[core, y], abuf.at[core, y], ay_s.at[i], ay_r.at[y], y_peer(i)[1])
    send(abuf.at[core, y], abuf.at[core, y], ac_s.at[0], ac_r.at[y], core_peer)
    for i in range(Y - 1, 0, -1):
        other, _ = y_peer(i)
        drain(abuf.at[core, other], ay_r.at[other])
        send(abuf.at[core, other], abuf.at[core, other], ac_s.at[i], ac_r.at[other], core_peer)
    for s in range(Y):
        drain(abuf.at[1 - core, s], ac_r.at[s])

    gathered = jnp.concatenate([abuf[p // Y, p % Y] for p in range(PL)], axis=0)
    chosen = jnp.dot(choose, gathered, preferred_element_type=F32)
    rows = chosen[ZK : 2 * ZK, 0:W] + jnp.dot(
        chosen[0:ZK, 0 : PL * FL].astype(BF16), down, preferred_element_type=F32
    )

    for s in range(Z):
        zsend[s] = rows[s * K : (s + 1) * K, :].astype(BF16)
    zrecv[z] = zsend[z]

    def scatter(i):
        other, device = z_peer(i)
        send(zsend.at[other], zrecv.at[z], fz_s, fz_r, device)

    each(Z, scatter)
    drain(hbuf.at[pl.ds(0, T - 1)], hd_s)
    for i in range(1, Y):
        drain(abuf.at[core, y], ay_s.at[i])
    for i in range(Y):
        drain(abuf.at[core, y], ac_s.at[i])
    drain(zrecv.at[pl.ds(0, Z - 1)], fz_r)
    final = zrecv[0].astype(F32)
    for s in range(1, Z):
        final = final + zrecv[s].astype(F32)
    out_ref[...] = (final + vector(db_ref)).astype(BF16)
    drain(zsend.at[pl.ds(0, Z - 1)], fz_s)


def chip_grid(devices):
    cores = 2
    along_y = 4 if devices >= 32 else 2
    return devices // (along_y * cores), along_y, cores


def per_device(
    query,
    key_new,
    value_new,
    resid,
    lengths,
    owner,
    page_table,
    kv_pool,
    out_weight,
    out_bias,
    norm_gain,
    norm_bias,
    up_weight_t,
    up_bias,
    down_weight,
    down_bias,
    order,
):
    K, W = query.shape
    devices = lax.axis_size("req")
    T = lax.axis_size("tp")
    Z, Y, C = chip_grid(devices)
    PL = Y * C
    R = devices * K
    D = W * T
    FL = up_weight_t.shape[0]
    pages, page_len = kv_pool.shape[1], kv_pool.shape[2]
    tokens = pages * page_len
    vmem = pl.BlockSpec(memory_space=pltpu.VMEM)
    hbm = pl.BlockSpec(memory_space=pltpu.HBM)
    dma = pltpu.SemaphoreType.DMA
    return pl.pallas_call(
        functools.partial(layer_kernel, (Z, Y, C, T, W, K)),
        out_shape=jax.ShapeDtypeStruct((K, W), BF16),
        in_specs=[hbm] * 17,
        out_specs=vmem,
        scratch_shapes=[
            pltpu.VMEM((K, W), BF16),
            pltpu.VMEM((K, W), BF16),
            pltpu.VMEM((3, 1, R), jnp.int32),
            pltpu.VMEM((page_table.shape[1], R), jnp.int32),
            pltpu.VMEM((W,), BF16),
            pltpu.VMEM((W,), BF16),
            pltpu.VMEM((W,), BF16),
            pltpu.VMEM((FL,), BF16),
            pltpu.VMEM((W,), BF16),
            pltpu.VMEM((2, tokens, W), BF16),
            pltpu.VMEM((W, D), BF16),
            pltpu.VMEM((PL, 2 * FL + 8, W), BF16),
            pltpu.VMEM((Z, K, W + HD), BF16),
            pltpu.VMEM((Z, K, 2 * W), BF16),
            pltpu.VMEM((PL, K, W + HD), BF16),
            pltpu.VMEM((PL, K, W + HD), BF16),
            pltpu.VMEM((PL, K, 2 * W), BF16),
            pltpu.VMEM((PL, K, 2 * W), BF16),
            pltpu.VMEM((Z * K, W + HD), F32),
            pltpu.VMEM((Z * K, 2 * W), F32),
            pltpu.VMEM((T, K, D), F32),
            pltpu.VMEM((K, D), F32),
            pltpu.VMEM((Z, K, W), BF16),
            pltpu.VMEM((Z * K, W), F32),
            pltpu.VMEM((T, Z * K, PL * FL), BF16),
            pltpu.VMEM((C, Y, Z * K + 8, W), BF16),
            pltpu.VMEM((Z, K, W), BF16),
            pltpu.VMEM((Z, K, W), BF16),
            dma((18,)),
        ]
        + [dma(())] * 14
        + [dma((Y,))] * 8
        + [dma(())] * 2,
        compiler_params=pltpu.CompilerParams(
            collective_id=0, has_side_effects=True, vmem_limit_bytes=60 * 1024 * 1024
        ),
    )(
        query,
        key_new,
        value_new,
        resid,
        owner.reshape(1, R),
        order.reshape(1, R),
        lengths.reshape(1, R),
        page_table.T,
        kv_pool.reshape(2, tokens, W),
        out_weight,
        up_weight_t,
        down_weight,
        out_bias,
        norm_gain,
        norm_bias,
        up_bias,
        down_bias,
    )


def solution(mesh):
    in_specs = (
        P("req", "tp"),
        P("req", "tp"),
        P("req", "tp"),
        P("req", "tp"),
        P(),
        P(),
        P(),
        P(None, "req", None, "tp"),
        P("tp", None),
        P("tp"),
        P("tp"),
        P("tp"),
        P("req", "tp"),
        P("req"),
        P("req", "tp"),
        P("tp"),
        P(),
    )
    return jax.shard_map(
        per_device, mesh=mesh, in_specs=in_specs, out_specs=P("req", "tp"), check_vma=False
    )
```

time: 84.9 us -> 63.7 us (0.75)
  local copies, waits for them, and re-layouts: 12.3 us -> 1.28 us
  Pallas kernels: 70.6 us -> 62.3 us
  other arithmetic: 1.44 us -> 0 us
    pallas_call x1, Pallas kernels: 70.6 us -> 62.3 us  [per_device(): pl.pallas_call(functools.partial(layer_kernel, (Z, Y, C, T, W, K)), out_s...]
    unnamed x18 -> x1, local copies, waits for them, and re-layouts: 8.85 us -> 1.28 us
    another operation x6 -> x0, local copies, waits for them, and re-layouts: 2.77 us -> none  [per_device(): jnp.stack([out_bias, norm_gain, norm_bias, down_bias, jnp.pad(up_bias, (0...]
where the time goes in v2:
time: 63.7 us; the launch traced here: 63.6 us
  Pallas kernels  62.3 us (98%)
  local copies, waits for them, and re-layouts  1.28 us (2%)
    pallas_call x1, Pallas kernels, per_device(): pl.pallas_call(functools.partial(layer_kernel, (Z, Y, C, T, W, K)), out_s...  62.3 us
    unnamed x1, local copies, waits for them, and re-layouts  1.28 us

profile of v2, /device:TPU:1, one launch (start us, length us, event | category | flops | bytes accessed | tf_op | source)
XLA Modules:
  0.0 63.6 jit_solution(10213413239988031634)
XLA Ops:
  0.0 62.3 %shard_map.163 = bf16[4,512]{1,0:T(4,128)(2,1)} custom-call(bf16[4,512]{1,0:T(4,128)(2,1)} %q_hbm.1, bf16[4,512]{1,0:T(4,128)(2,1)} %k_hbm.1, bf16[4,512]{1,0:T(4,128)(2,1)} %v_hbm.1, bf16[4,512]{1,0:T(4,128)(2,1)} %res_hbm.1, s32[1,512]{1,0:T(1,128)} %bitcast.7, s32[1,512]{1,0:T(1,128)} %bitcast.8, s32[1,512]{1,0:T(1,128)} %bitcast.9, s32[16,512]{1,0:T(8,128)} %bitcast.6, ...), custom_call_target="tpu_custom_call" | custom-call | tf_op jit(solution)/shard_map/pallas_call | solution.py:547
  62.3 1.3 %copy.19 = bf16[4,512]{1,0:T(4,128)(2,1)} copy(bf16[4,512]{1,0:T(4,128)(2,1)} %shard_map.163) | data formatting | bytes 8192

commit v3 on v2

--- a/solution.py
+++ b/solution.py
@@ -65,12 +65,16 @@
     wts,
     g0,
     g1,
+    g2,
     p0,
+    p1,
+    p2,
     r0,
-    p1,
     r1,
+    r2,
     a0,
     a1,
+    a2,
     part,
     stream,
     nbuf,
@@ -80,14 +84,13 @@
     zsend,
     zrecv,
     local_sem,
-    zq_s,
-    zq_r,
-    zv_s,
-    zv_r,
-    pq_s,
-    pq_r,
-    pv_s,
-    pv_r,
+    near_s,
+    below_r,
+    above_r,
+    far_s,
+    far_r,
+    plane_s,
+    plane_r,
     pt_s,
     pt_r,
     ng_s,
@@ -113,6 +116,8 @@
     ZK = Z * K
     FL = up_hbm.shape[0]
     BLK = ZK + 8
+    MID = Z // 2
+    REACH = Z // 4
     me = lax.axis_index("req")
     t = lax.axis_index("tp")
     core = lax.rem(me, C)
@@ -123,9 +128,12 @@
     def far_first(i, n):
         return n // 2 + (i // 2) * (1 - 2 * (i % 2))
 
+    def z_away(d):
+        return {"req": lax.rem(z + d + Z, Z) * PL + pid}
+
     def z_peer(i):
-        other = lax.rem(z + far_first(i, Z), Z)
-        return other, {"req": other * PL + pid}
+        d = far_first(i, Z)
+        return d, z_away(d)
 
     plane_steps = sorted(
         [(a, b) for a in range(Y) for b in range(C) if a or b],
@@ -170,9 +178,9 @@
     pairs = [
         (q_hbm, q_ref),
         (k_hbm, k_ref),
-        (q_hbm, g0.at[z, :, pl.ds(0, W)]),
-        (v_hbm, g1.at[z, :, pl.ds(0, W)]),
-        (res_hbm, g1.at[z, :, pl.ds(W, W)]),
+        (q_hbm, g0.at[MID, :, pl.ds(0, W)]),
+        (v_hbm, g1.at[MID]),
+        (res_hbm, g2.at[MID]),
         (owner_hbm, meta_ref.at[0]),
         (order_hbm, meta_ref.at[1]),
         (len_hbm, meta_ref.at[2]),
@@ -202,7 +210,9 @@
 
         return body
 
-    each(Z, greet(z_peer))
+    near = [d for r in range(REACH, 0, -1) for d in (r, -r)]
+    for d in near:
+        greet(lambda d: (d, z_away(d)))(d)
     for step in plane_steps:
         greet(plane_peer)(step)
     each(T, greet(tp_peer))
@@ -224,14 +234,32 @@
         packed = jnp.where(lane == h, high, packed)
         packed = jnp.where(lane == H + h, mid, packed)
         packed = jnp.where(lane == 2 * H + h, low, packed)
-    g0[z, :, W : W + HD] = packed.astype(BF16)
+    g0[MID, :, W : W + HD] = packed.astype(BF16)
 
     for load in loads[2:5]:
         load.wait()
-    pl.semaphore_wait(barrier, (Z - 1) + (PL - 1) + (T - 1))
-
-    each(Z, lambda d: send(g0.at[z], g0.at[z], zq_s, zq_r, z_peer(d)[1]))
-    each(Z, lambda d: send(g1.at[z], g1.at[z], zv_s, zv_r, z_peer(d)[1]))
+    pl.semaphore_wait(barrier, len(near) + (PL - 1) + (T - 1))
+
+    sources = (g0, g1, g2)
+    for n, source in enumerate(sources):
+        for d in near:
+            sem = below_r.at[n] if d > 0 else above_r.at[n]
+            send(source.at[MID], source.at[MID - d], near_s.at[n], sem, z_away(d))
+
+    def pass_on(n):
+        source = sources[n]
+        below = source.at[pl.ds(MID - REACH, REACH)]
+        drain(below, below_r.at[n])
+        send(below, source.at[pl.ds(MID - 2 * REACH, REACH)], far_s.at[n], far_r.at[n], z_away(REACH))
+        drain(source.at[pl.ds(MID + 1, REACH)], above_r.at[n])
+        if REACH > 1:
+            send(
+                source.at[pl.ds(MID + 1, REACH - 1)],
+                source.at[pl.ds(MID + 1 + REACH, REACH - 1)],
+                far_s.at[n],
+                far_r.at[n],
+                z_away(-REACH),
+            )
 
     for load in [loads[11], loads[12], loads[16]]:
         load.wait()
@@ -269,7 +297,10 @@
 
     KL = max(ZK, HD)
     kap = iota((1, KL), 1)
-    kap_request = over(kap, K) * (PL * K) + pid * K + within(kap, K)
+    kap_request = (
+        within(over(kap, K) + z + MID, Z) * (PL * K) + pid * K + within(kap, K)
+    )
+    kap_request = jnp.where(kap < ZK, kap_request, -1)
     pick = hot(iota((R, KL), 0) == kap_request)
     sub8 = iota((8, R), 0)
 
@@ -288,31 +319,32 @@
     sort = hot(iota((PL * K, ZK), 0).astype(F32) == target)
     out_request = (picked[2:3, :] * 16.0 + picked[3:4, :]).astype(jnp.int32)
 
-    def to_plane(source, flat, sendbuf, recvbuf, zs, zr, ps, pr):
-        drain(source.at[pl.ds(0, Z - 1)], zr)
+    for n in range(3):
+        pass_on(n)
+
+    def to_plane(n, flat, sendbuf, recvbuf):
+        source = sources[n]
+        drain(source.at[pl.ds(0, 2 * REACH - 1)], far_r.at[n])
         for s in range(Z):
             flat[s * K : (s + 1) * K, :] = source[s].astype(F32)
         rows = jnp.dot(sort, flat[...].astype(BF16), preferred_element_type=F32)
         for d in range(PL):
             sendbuf[d] = rows[d * K : (d + 1) * K, :].astype(BF16)
         recvbuf[pid] = sendbuf[pid]
-
-        def body(step):
+        for step in plane_steps:
             other, device = plane_peer(step)
-            send(sendbuf.at[other], recvbuf.at[pid], ps, pr, device)
-
-        for step in plane_steps:
-            body(step)
-        drain(source.at[pl.ds(0, Z - 1)], zs)
-
-    def from_plane(recvbuf, pr):
-        drain(recvbuf.at[pl.ds(0, PL - 1)], pr)
+            send(sendbuf.at[other], recvbuf.at[pid], plane_s.at[n], plane_r.at[n], device)
+        drain(source.at[pl.ds(0, 2 * REACH)], near_s.at[n])
+        drain(source.at[pl.ds(0, 2 * REACH - 1)], far_s.at[n])
+
+    def from_plane(n, recvbuf):
+        drain(recvbuf.at[pl.ds(0, PL - 1)], plane_r.at[n])
         total = recvbuf[0].astype(F32)
         for s in range(1, PL):
             total = total + recvbuf[s].astype(F32)
         return total
 
-    to_plane(g0, a0, p0, r0, zq_s, zq_r, pq_s, pq_r)
+    to_plane(0, a0, p0, r0)
     for i in range(1, Y):
         other, _ = y_peer(i)
         arrived = wts.at[other * C + core]
@@ -343,9 +375,10 @@
         valid = jnp.where(hit, 1.0, valid)
     valid = valid > 0.5
 
-    to_plane(g1, a1, p1, r1, zv_s, zv_r, pv_s, pv_r)
-
-    own0 = from_plane(r0, pq_r)
+    to_plane(1, a1, p1, r1)
+    to_plane(2, a2, p2, r2)
+
+    own0 = from_plane(0, r0)
     q_own = own0[:, 0:W]
     head_of_row = over(iota((H * K, W), 0), K)
     head_of_lane = over(iota((H * K, W), 1), HD)
@@ -377,7 +410,7 @@
     for h in range(1, H):
         numer = numer + wide[:, h * HD : (h + 1) * HD]
 
-    own1 = from_plane(r1, pv_r)
+    own1 = from_plane(1, r1)
     v_fold = jnp.concatenate([own1[:, h * HD : (h + 1) * HD] for h in range(H)], axis=0)
     numer = numer + self_weight.astype(BF16).astype(F32) * v_fold
     attn_fold = numer / total
@@ -388,9 +421,10 @@
     loads[10].wait()
     for load in [loads[13], loads[14], loads[15], loads[17]]:
         load.wait()
+    own2 = from_plane(2, r2)
     part[t] = jnp.dot(attn, ow[...], preferred_element_type=F32)
     here = pl.ds(pl.multiple_of(t * W, W), W)
-    part[t, :, here] = part[t, :, here] + (own1[:, W : 2 * W] + vector(ob_ref))
+    part[t, :, here] = part[t, :, here] + (own2 + vector(ob_ref))
     each(T, lambda d: send(part.at[t], part.at[t], pt_s, pt_r, tp_peer(d)[1]))
     drain(part.at[pl.ds(0, T - 1)], pt_r)
     summed = part[0]
@@ -403,16 +437,20 @@
     inverse = lax.rsqrt(var + EPS)
     stream[...] = rows_f
     mine_f32 = stream[:, here]
-    nbuf[z] = ((mine_f32 - mean) * inverse * vector(ng_ref) + vector(nb_ref)).astype(BF16)
-
-    each(Z, lambda d: send(nbuf.at[z], nbuf.at[z], ng_s, ng_r, z_peer(d)[1]))
+    nbuf[MID] = ((mine_f32 - mean) * inverse * vector(ng_ref) + vector(nb_ref)).astype(BF16)
+
+    def spread_rows(i):
+        d, device = z_peer(i)
+        send(nbuf.at[MID], nbuf.at[lax.rem(MID - d + Z, Z)], ng_s, ng_r, device)
+
+    each(Z, spread_rows)
 
     found = jnp.dot(
         stacked(owner_row, rank_row), hot(iota((R, KL), 0) == out_request), preferred_element_type=F32
     )
     home = found[0:1, :].astype(jnp.int32)
     block = (within(home, C) * Y + within(over(home, C), Y)) * BLK + found[1:2, :].astype(jnp.int32)
-    row_at = block + over(home, PL) * K
+    row_at = block + within(over(home, PL) - z + MID + Z, Z) * K
     stream_at = jnp.where(over(home, PL) == z, block + ZK, -1)
     at8 = jnp.where(
         iota((8, KL), 0) == 0,
@@ -427,8 +465,8 @@
     abuf[core, y, ZK:BLK, :] = jnp.concatenate(
         [mine_f32, jnp.zeros((BLK - ZK - K, W), F32)], axis=0
     ).astype(BF16)
-    drain(p0.at[pl.ds(0, PL - 1)], pq_s)
-    drain(p1.at[pl.ds(0, PL - 1)], pv_s)
+    for n, sendbuf in enumerate((p0, p1, p2)):
+        drain(sendbuf.at[pl.ds(0, PL - 1)], plane_s.at[n])
     drain(part.at[pl.ds(0, T - 1)], pt_s)
 
     drain(nbuf.at[pl.ds(0, Z - 1)], ng_r)
@@ -486,11 +524,13 @@
 
     for s in range(Z):
         zsend[s] = rows[s * K : (s + 1) * K, :].astype(BF16)
-    zrecv[z] = zsend[z]
+    zrecv[MID] = zsend[MID]
 
     def scatter(i):
-        other, device = z_peer(i)
-        send(zsend.at[other], zrecv.at[z], fz_s, fz_r, device)
+        d, device = z_peer(i)
+        send(
+            zsend.at[lax.rem(MID + d, Z)], zrecv.at[lax.rem(MID - d + Z, Z)], fz_s, fz_r, device
+        )
 
     each(Z, scatter)
     drain(hbuf.at[pl.ds(0, T - 1)], hd_s)
@@ -563,13 +603,17 @@
             pltpu.VMEM((W, D), BF16),
             pltpu.VMEM((PL, 2 * FL + 8, W), BF16),
             pltpu.VMEM((Z, K, W + HD), BF16),
-            pltpu.VMEM((Z, K, 2 * W), BF16),
+            pltpu.VMEM((Z, K, W), BF16),
+            pltpu.VMEM((Z, K, W), BF16),
             pltpu.VMEM((PL, K, W + HD), BF16),
+            pltpu.VMEM((PL, K, W), BF16),
+            pltpu.VMEM((PL, K, W), BF16),
             pltpu.VMEM((PL, K, W + HD), BF16),
-            pltpu.VMEM((PL, K, 2 * W), BF16),
-            pltpu.VMEM((PL, K, 2 * W), BF16),
+            pltpu.VMEM((PL, K, W), BF16),
+            pltpu.VMEM((PL, K, W), BF16),
             pltpu.VMEM((Z * K, W + HD), F32),
-            pltpu.VMEM((Z * K, 2 * W), F32),
+            pltpu.VMEM((Z * K, W), F32),
+            pltpu.VMEM((Z * K, W), F32),
             pltpu.VMEM((T, K, D), F32),
             pltpu.VMEM((K, D), F32),
             pltpu.VMEM((Z, K, W), BF16),
@@ -580,7 +624,8 @@
             pltpu.VMEM((Z, K, W), BF16),
             dma((18,)),
         ]
-        + [dma(())] * 14
+        + [dma((3,))] * 7
+        + [dma(())] * 6
         + [dma((Y,))] * 8
         + [dma(())] * 2,
         compiler_params=pltpu.CompilerParams(

time: 63.7 us -> 62.4 us (0.980)
  Pallas kernels: 62.3 us -> 60.9 us
    pallas_call x1, Pallas kernels: 62.3 us -> 60.9 us  [per_device(): pl.pallas_call(functools.partial(layer_kernel, (Z, Y, C, T, W, K)), out_s...]
where the time goes in v3:
time: 62.4 us; the launch traced here: 62.2 us
  Pallas kernels  60.9 us (98%)
  local copies, waits for them, and re-layouts  1.28 us (2%)
    pallas_call x1, Pallas kernels, per_device(): pl.pallas_call(functools.partial(layer_kernel, (Z, Y, C, T, W, K)), out_s...  60.9 us
    unnamed x1, local copies, waits for them, and re-layouts  1.28 us

profile of v3, /device:TPU:1, one launch (start us, length us, event | category | flops | bytes accessed | tf_op | source)
XLA Modules:
  0.0 62.2 jit_solution(14303057531140290709)
XLA Ops:
  0.0 60.9 %shard_map.163 = bf16[4,512]{1,0:T(4,128)(2,1)} custom-call(bf16[4,512]{1,0:T(4,128)(2,1)} %q_hbm.1, bf16[4,512]{1,0:T(4,128)(2,1)} %k_hbm.1, bf16[4,512]{1,0:T(4,128)(2,1)} %v_hbm.1, bf16[4,512]{1,0:T(4,128)(2,1)} %res_hbm.1, s32[1,512]{1,0:T(1,128)} %bitcast.7, s32[1,512]{1,0:T(1,128)} %bitcast.8, s32[1,512]{1,0:T(1,128)} %bitcast.9, s32[16,512]{1,0:T(8,128)} %bitcast.6, ...), custom_call_target="tpu_custom_call" | custom-call | tf_op jit(solution)/shard_map/pallas_call | solution.py:587
  60.9 1.3 %copy.19 = bf16[4,512]{1,0:T(4,128)(2,1)} copy(bf16[4,512]{1,0:T(4,128)(2,1)} %shard_map.163) | data formatting | bytes 8192

commit v4 on v3

--- a/solution.py
+++ b/solution.py
@@ -53,6 +53,8 @@
     out_ref,
     q_ref,
     k_ref,
+    v_ref,
+    res_ref,
     meta_ref,
     table_ref,
     ob_ref,
@@ -65,16 +67,10 @@
     wts,
     g0,
     g1,
-    g2,
     p0,
     p1,
-    p2,
     r0,
     r1,
-    r2,
-    a0,
-    a1,
-    a2,
     part,
     stream,
     nbuf,
@@ -85,8 +81,10 @@
     zrecv,
     local_sem,
     near_s,
-    below_r,
-    above_r,
+    low_r,
+    high_r,
+    low_edge_r,
+    high_edge_r,
     far_s,
     far_r,
     plane_s,
@@ -115,6 +113,7 @@
     D = W * T
     ZK = Z * K
     FL = up_hbm.shape[0]
+    HALF = ZK // 2
     BLK = ZK + 8
     MID = Z // 2
     REACH = Z // 4
@@ -178,9 +177,8 @@
     pairs = [
         (q_hbm, q_ref),
         (k_hbm, k_ref),
-        (q_hbm, g0.at[MID, :, pl.ds(0, W)]),
-        (v_hbm, g1.at[MID]),
-        (res_hbm, g2.at[MID]),
+        (v_hbm, v_ref),
+        (res_hbm, res_ref),
         (owner_hbm, meta_ref.at[0]),
         (order_hbm, meta_ref.at[1]),
         (len_hbm, meta_ref.at[2]),
@@ -221,8 +219,8 @@
         load.start()
 
     scale = 1.0 / math.sqrt(HD)
-    loads[0].wait()
-    loads[1].wait()
+    for load in loads[0:4]:
+        load.wait()
     product = q_ref[...].astype(F32) * k_ref[...].astype(F32)
     lane = lax.broadcasted_iota(jnp.int32, (K, HD), 1)
     packed = jnp.zeros((K, HD), F32)
@@ -234,34 +232,40 @@
         packed = jnp.where(lane == h, high, packed)
         packed = jnp.where(lane == H + h, mid, packed)
         packed = jnp.where(lane == 2 * H + h, low, packed)
-    g0[MID, :, W : W + HD] = packed.astype(BF16)
-
-    for load in loads[2:5]:
-        load.wait()
+    g0[MID] = jnp.concatenate(
+        [
+            jnp.concatenate([q_ref[...].astype(F32), packed], axis=1),
+            jnp.concatenate([v_ref[...].astype(F32), jnp.zeros((K, HD), F32)], axis=1),
+        ],
+        axis=0,
+    ).astype(BF16)
+    own_rest = res_ref[...].astype(F32)
+    g1[MID] = jnp.concatenate([own_rest[:, 0 : W // 2], own_rest[:, W // 2 : W]], axis=0).astype(
+        BF16
+    )
+
     pl.semaphore_wait(barrier, len(near) + (PL - 1) + (T - 1))
 
-    sources = (g0, g1, g2)
+    sources = (g0, g1)
     for n, source in enumerate(sources):
         for d in near:
-            sem = below_r.at[n] if d > 0 else above_r.at[n]
+            if abs(d) == REACH:
+                sem = low_edge_r.at[n] if d > 0 else high_edge_r.at[n]
+            else:
+                sem = low_r.at[n] if d > 0 else high_r.at[n]
             send(source.at[MID], source.at[MID - d], near_s.at[n], sem, z_away(d))
 
     def pass_on(n):
         source = sources[n]
-        below = source.at[pl.ds(MID - REACH, REACH)]
-        drain(below, below_r.at[n])
-        send(below, source.at[pl.ds(MID - 2 * REACH, REACH)], far_s.at[n], far_r.at[n], z_away(REACH))
-        drain(source.at[pl.ds(MID + 1, REACH)], above_r.at[n])
-        if REACH > 1:
-            send(
-                source.at[pl.ds(MID + 1, REACH - 1)],
-                source.at[pl.ds(MID + 1 + REACH, REACH - 1)],
-                far_s.at[n],
-                far_r.at[n],
-                z_away(-REACH),
-            )
-
-    for load in [loads[11], loads[12], loads[16]]:
+        low, high = source.at[MID - REACH], source.at[MID + REACH]
+        drain(low, low_edge_r.at[n])
+        for e in range(REACH, 0, -1):
+            send(low, source.at[MID - REACH - e], far_s.at[n], far_r.at[n], z_away(e))
+        drain(high, high_edge_r.at[n])
+        for e in range(REACH - 1, 0, -1):
+            send(high, source.at[MID + REACH + e], far_s.at[n], far_r.at[n], z_away(-e))
+
+    for load in [loads[10], loads[11], loads[15]]:
         load.wait()
     spread = hot(iota((FL, W), 1) == pid * FL + iota((FL, W), 0))
     bias8 = jnp.where(iota((8, FL), 0) == 0, vector(ub_ref), 0.0)
@@ -272,7 +276,7 @@
         send(wts.at[pid], wts.at[pid], wy_s.at[i], wy_r.at[y], y_peer(i)[1])
     send(wts.at[pid], wts.at[pid], wc_s.at[0], wc_r.at[y], core_peer)
 
-    for load in loads[5:9]:
+    for load in loads[4:8]:
         load.wait()
     owner_i = meta_ref[0]
     owner_row = owner_i.astype(F32)
@@ -297,11 +301,11 @@
 
     KL = max(ZK, HD)
     kap = iota((1, KL), 1)
-    kap_request = (
-        within(over(kap, K) + z + MID, Z) * (PL * K) + pid * K + within(kap, K)
-    )
-    kap_request = jnp.where(kap < ZK, kap_request, -1)
-    pick = hot(iota((R, KL), 0) == kap_request)
+    out_of = within(over(kap, K) + z - REACH + Z, Z) * (PL * K) + pid * K + within(kap, K)
+    pick_out = hot(iota((R, KL), 0) == jnp.where(kap < ZK, out_of, -1))
+    tall = iota((1, 2 * ZK), 1)
+    row_of = within(over(tall, 2 * K) + z + MID, Z) * (PL * K) + pid * K + within(tall, K)
+    pick_row = hot(iota((R, 2 * ZK), 0) == row_of)
     sub8 = iota((8, R), 0)
 
     def stacked(*rows):
@@ -310,26 +314,32 @@
             total = jnp.where(sub8 == i, row.astype(F32), total)
         return total.astype(BF16)
 
-    picked = jnp.dot(
-        stacked(owner_row, rank_row, over(order_i, 16), within(order_i, 16)),
-        pick,
-        preferred_element_type=F32,
-    )
-    target = picked[0:1, 0:ZK] * K + picked[1:2, 0:ZK] - (z * (PL * K)).astype(F32)
-    sort = hot(iota((PL * K, ZK), 0).astype(F32) == target)
-    out_request = (picked[2:3, :] * 16.0 + picked[3:4, :]).astype(jnp.int32)
-
-    for n in range(3):
+    picked = jnp.dot(stacked(owner_row, rank_row), pick_row, preferred_element_type=F32)
+    target = (
+        (picked[0:1, :] - (z * PL).astype(F32)) * (2 * K)
+        + picked[1:2, :]
+        + (within(over(tall, K), 2) * K).astype(F32)
+    )
+    sort = hot(iota((PL * 2 * K, 2 * ZK), 0).astype(F32) == target)
+    ordered = jnp.dot(
+        stacked(over(order_i, 16), within(order_i, 16)), pick_out, preferred_element_type=F32
+    )
+    out_request = (ordered[0:1, :] * 16.0 + ordered[1:2, :]).astype(jnp.int32)
+
+    for n in range(2):
         pass_on(n)
 
-    def to_plane(n, flat, sendbuf, recvbuf):
+    def to_plane(n, sendbuf, recvbuf):
         source = sources[n]
+        if REACH > 1:
+            drain(source.at[pl.ds(MID - REACH + 1, REACH - 1)], low_r.at[n])
+            drain(source.at[pl.ds(MID + 1, REACH - 1)], high_r.at[n])
         drain(source.at[pl.ds(0, 2 * REACH - 1)], far_r.at[n])
-        for s in range(Z):
-            flat[s * K : (s + 1) * K, :] = source[s].astype(F32)
-        rows = jnp.dot(sort, flat[...].astype(BF16), preferred_element_type=F32)
+        rows = jnp.dot(
+            sort, source[...].reshape(2 * ZK, source.shape[2]), preferred_element_type=F32
+        ).astype(BF16)
         for d in range(PL):
-            sendbuf[d] = rows[d * K : (d + 1) * K, :].astype(BF16)
+            sendbuf[d] = rows[d * 2 * K : (d + 1) * 2 * K, :]
         recvbuf[pid] = sendbuf[pid]
         for step in plane_steps:
             other, device = plane_peer(step)
@@ -344,7 +354,7 @@
             total = total + recvbuf[s].astype(F32)
         return total
 
-    to_plane(0, a0, p0, r0)
+    to_plane(0, p0, r0)
     for i in range(1, Y):
         other, _ = y_peer(i)
         arrived = wts.at[other * C + core]
@@ -375,11 +385,11 @@
         valid = jnp.where(hit, 1.0, valid)
     valid = valid > 0.5
 
-    to_plane(1, a1, p1, r1)
-    to_plane(2, a2, p2, r2)
+    to_plane(1, p1, r1)
 
     own0 = from_plane(0, r0)
-    q_own = own0[:, 0:W]
+    q_own = own0[0:K, 0:W]
+    v_own = own0[K : 2 * K, 0:W]
     head_of_row = over(iota((H * K, W), 0), K)
     head_of_lane = over(iota((H * K, W), 1), HD)
     q_block = jnp.where(
@@ -387,14 +397,14 @@
     ).astype(BF16)
     self_col = jnp.concatenate(
         [
-            own0[:, W + h : W + h + 1]
-            + own0[:, W + H + h : W + H + h + 1]
-            + own0[:, W + 2 * H + h : W + 2 * H + h + 1]
+            own0[0:K, W + h : W + h + 1]
+            + own0[0:K, W + H + h : W + H + h + 1]
+            + own0[0:K, W + 2 * H + h : W + 2 * H + h + 1]
             for h in range(H)
         ],
         axis=0,
     )
-    loads[9].wait()
+    loads[8].wait()
     scores = (
         lax.dot_general(q_block, kv[0], (((1,), (1,)), ((), ())), preferred_element_type=F32)
         * scale
@@ -410,21 +420,21 @@
     for h in range(1, H):
         numer = numer + wide[:, h * HD : (h + 1) * HD]
 
-    own1 = from_plane(1, r1)
-    v_fold = jnp.concatenate([own1[:, h * HD : (h + 1) * HD] for h in range(H)], axis=0)
+    v_fold = jnp.concatenate([v_own[:, h * HD : (h + 1) * HD] for h in range(H)], axis=0)
     numer = numer + self_weight.astype(BF16).astype(F32) * v_fold
     attn_fold = numer / total
     attn = jnp.concatenate([attn_fold[h * K : (h + 1) * K, :] for h in range(H)], axis=1).astype(
         BF16
     )
 
-    loads[10].wait()
-    for load in [loads[13], loads[14], loads[15], loads[17]]:
+    loads[9].wait()
+    for load in [loads[12], loads[13], loads[14], loads[16]]:
         load.wait()
-    own2 = from_plane(2, r2)
     part[t] = jnp.dot(attn, ow[...], preferred_element_type=F32)
+    own1 = from_plane(1, r1)
+    res_own = jnp.concatenate([own1[0:K], own1[K : 2 * K]], axis=1)
     here = pl.ds(pl.multiple_of(t * W, W), W)
-    part[t, :, here] = part[t, :, here] + (own2 + vector(ob_ref))
+    part[t, :, here] = part[t, :, here] + (res_own + vector(ob_ref))
     each(T, lambda d: send(part.at[t], part.at[t], pt_s, pt_r, tp_peer(d)[1]))
     drain(part.at[pl.ds(0, T - 1)], pt_r)
     summed = part[0]
@@ -437,21 +447,21 @@
     inverse = lax.rsqrt(var + EPS)
     stream[...] = rows_f
     mine_f32 = stream[:, here]
-    nbuf[MID] = ((mine_f32 - mean) * inverse * vector(ng_ref) + vector(nb_ref)).astype(BF16)
-
-    def spread_rows(i):
+    nbuf[REACH] = ((mine_f32 - mean) * inverse * vector(ng_ref) + vector(nb_ref)).astype(BF16)
+
+    for i in range(1, Z):
         d, device = z_peer(i)
-        send(nbuf.at[MID], nbuf.at[lax.rem(MID - d + Z, Z)], ng_s, ng_r, device)
-
-    each(Z, spread_rows)
+        far = 1 if REACH < d < Z - REACH + 1 else 0
+        send(nbuf.at[REACH], nbuf.at[(REACH - d) % Z], ng_s, ng_r.at[far], device)
 
     found = jnp.dot(
         stacked(owner_row, rank_row), hot(iota((R, KL), 0) == out_request), preferred_element_type=F32
     )
     home = found[0:1, :].astype(jnp.int32)
     block = (within(home, C) * Y + within(over(home, C), Y)) * BLK + found[1:2, :].astype(jnp.int32)
-    row_at = block + within(over(home, PL) - z + MID + Z, Z) * K
-    stream_at = jnp.where(over(home, PL) == z, block + ZK, -1)
+    away = within(over(home, PL) - z + REACH + Z, Z) * K
+    row_at = block + away + jnp.where(away < HALF, 0, 8)
+    stream_at = jnp.where(over(home, PL) == z, block + HALF, -1)
     at8 = jnp.where(
         iota((8, KL), 0) == 0,
         row_at.astype(F32),
@@ -462,16 +472,12 @@
     choose = jnp.concatenate(
         [hot(lane_a == at_col[:, 0:1]), hot(lane_a == at_col[:, 1:2])], axis=0
     )
-    abuf[core, y, ZK:BLK, :] = jnp.concatenate(
-        [mine_f32, jnp.zeros((BLK - ZK - K, W), F32)], axis=0
+    abuf[core, y, HALF : HALF + 8, :] = jnp.concatenate(
+        [mine_f32, jnp.zeros((8 - K, W), F32)], axis=0
     ).astype(BF16)
-    for n, sendbuf in enumerate((p0, p1, p2)):
+    for n, sendbuf in enumerate((p0, p1)):
         drain(sendbuf.at[pl.ds(0, PL - 1)], plane_s.at[n])
-    drain(part.at[pl.ds(0, T - 1)], pt_s)
-
-    drain(nbuf.at[pl.ds(0, Z - 1)], ng_r)
-    for s in range(Z):
-        x32[s * K : (s + 1) * K, :] = nbuf[s].astype(F32)
+
     for i in range(1, Y + 1):
         if i < Y:
             other, _ = y_peer(i)
@@ -482,11 +488,23 @@
         drain(wts.at[arrived], wc_r.at[other])
 
     up = jnp.concatenate([wts[p, 0:FL, :] for p in range(PL)], axis=0)
-    hidden = lax.dot_general(
-        x32[...].astype(BF16), up, (((1,), (1,)), ((), ())), preferred_element_type=F32
-    )
-    hbuf[t] = hidden.astype(BF16)
-    each(T, lambda d: send(hbuf.at[t], hbuf.at[t], hd_s, hd_r, tp_peer(d)[1]))
+    halves = (
+        (pl.ds(0, HALF), pl.ds(0, HALF + 8), pl.ds(0, HALF)),
+        (pl.ds(HALF, HALF), pl.ds(HALF + 8, HALF), pl.ds(HALF + 8, HALF)),
+    )
+    drain(part.at[pl.ds(0, T - 1)], pt_s)
+    for n, (rows_n, _, _) in enumerate(halves):
+        drain(nbuf.at[pl.ds(0, 2 * REACH - 1 + n)], ng_r.at[n])
+        first = n * (Z // 2)
+        for s in range(first, first + Z // 2):
+            x32[s * K : (s + 1) * K, :] = nbuf[s].astype(F32)
+        hidden = lax.dot_general(
+            x32[rows_n, :].astype(BF16), up, (((1,), (1,)), ((), ())), preferred_element_type=F32
+        )
+        hbuf[t, rows_n, :] = hidden.astype(BF16)
+        for i in range(1, T):
+            block_t = hbuf.at[t, rows_n]
+            send(block_t, block_t, hd_s.at[n], hd_r.at[n], tp_peer(i)[1])
     up_bias = wts[0, 2 * FL : 2 * FL + 8, :].astype(F32)
     for p in range(1, PL):
         up_bias = up_bias + wts[p, 2 * FL : 2 * FL + 8, :].astype(F32)
@@ -496,25 +514,29 @@
         drain(wts.at[pid], wy_s.at[i])
     for i in range(Y):
         drain(wts.at[pid], wc_s.at[i])
-    drain(hbuf.at[pl.ds(0, T - 1)], hd_r)
-    before = hbuf[0].astype(F32)
-    for s in range(1, T):
-        before = before + hbuf[s].astype(F32)
-    before = before + up_bias[0:1, 0 : PL * FL]
-    active = 0.5 * before * (1.0 + lax.erf(before * math.sqrt(0.5)))
-    abuf[core, y, 0:ZK, 0 : PL * FL] = active.astype(BF16)
-    if PL * FL < W:
-        abuf[core, y, 0:ZK, PL * FL : W] = jnp.zeros((ZK, W - PL * FL), BF16)
-
-    for i in range(1, Y):
-        send(abuf.at[core, y], abuf.at[core, y], ay_s.at[i], ay_r.at[y], y_peer(i)[1])
-    send(abuf.at[core, y], abuf.at[core, y], ac_s.at[0], ac_r.at[y], core_peer)
-    for i in range(Y - 1, 0, -1):
-        other, _ = y_peer(i)
-        drain(abuf.at[core, other], ay_r.at[other])
-        send(abuf.at[core, other], abuf.at[core, other], ac_s.at[i], ac_r.at[other], core_peer)
-    for s in range(Y):
-        drain(abuf.at[1 - core, s], ac_r.at[s])
+    for n, (rows_n, sent_n, at_n) in enumerate(halves):
+        drain(hbuf.at[pl.ds(0, T - 1), rows_n], hd_r.at[n])
+        before = hbuf[0, rows_n, :].astype(F32)
+        for s in range(1, T):
+            before = before + hbuf[s, rows_n, :].astype(F32)
+        before = before + up_bias[0:1, 0 : PL * FL]
+        active = 0.5 * before * (1.0 + lax.erf(before * math.sqrt(0.5)))
+        abuf[core, y, at_n, 0 : PL * FL] = active.astype(BF16)
+        if PL * FL < W:
+            abuf[core, y, at_n, PL * FL : W] = jnp.zeros((HALF, W - PL * FL), BF16)
+        own_block = abuf.at[core, y, sent_n]
+        for i in range(1, Y):
+            send(own_block, own_block, ay_s.at[n, i], ay_r.at[n, y], y_peer(i)[1])
+        send(own_block, own_block, ac_s.at[n, 0], ac_r.at[n, y], core_peer)
+    for n, (_, sent_n, _) in enumerate(halves):
+        for i in range(Y - 1, 0, -1):
+            other, _ = y_peer(i)
+            block_n = abuf.at[core, other, sent_n]
+            drain(block_n, ay_r.at[n, other])
+            send(block_n, block_n, ac_s.at[n, i], ac_r.at[n, other], core_peer)
+    for n, (_, sent_n, _) in enumerate(halves):
+        for s in range(Y):
+            drain(abuf.at[1 - core, s, sent_n], ac_r.at[n, s])
 
     gathered = jnp.concatenate([abuf[p // Y, p % Y] for p in range(PL)], axis=0)
     chosen = jnp.dot(choose, gathered, preferred_element_type=F32)
@@ -524,20 +546,16 @@
 
     for s in range(Z):
         zsend[s] = rows[s * K : (s + 1) * K, :].astype(BF16)
-    zrecv[MID] = zsend[MID]
-
-    def scatter(i):
+    zrecv[REACH] = zsend[REACH]
+    for i in range(1, Z):
         d, device = z_peer(i)
-        send(
-            zsend.at[lax.rem(MID + d, Z)], zrecv.at[lax.rem(MID - d + Z, Z)], fz_s, fz_r, device
-        )
-
-    each(Z, scatter)
-    drain(hbuf.at[pl.ds(0, T - 1)], hd_s)
-    for i in range(1, Y):
-        drain(abuf.at[core, y], ay_s.at[i])
-    for i in range(Y):
-        drain(abuf.at[core, y], ac_s.at[i])
+        send(zsend.at[(REACH + d) % Z], zrecv.at[(REACH - d) % Z], fz_s, fz_r, device)
+    for n, (rows_n, sent_n, _) in enumerate(halves):
+        drain(hbuf.at[pl.ds(0, T - 1), rows_n], hd_s.at[n])
+        for i in range(1, Y):
+            drain(abuf.at[core, y, sent_n], ay_s.at[n, i])
+        for i in range(Y):
+            drain(abuf.at[core, y, sent_n], ac_s.at[n, i])
     drain(zrecv.at[pl.ds(0, Z - 1)], fz_r)
     final = zrecv[0].astype(F32)
     for s in range(1, Z):
@@ -592,6 +610,8 @@
         scratch_shapes=[
             pltpu.VMEM((K, W), BF16),
             pltpu.VMEM((K, W), BF16),
+            pltpu.VMEM((K, W), BF16),
+            pltpu.VMEM((K, W), BF16),
             pltpu.VMEM((3, 1, R), jnp.int32),
             pltpu.VMEM((page_table.shape[1], R), jnp.int32),
             pltpu.VMEM((W,), BF16),
@@ -602,18 +622,12 @@
             pltpu.VMEM((2, tokens, W), BF16),
             pltpu.VMEM((W, D), BF16),
             pltpu.VMEM((PL, 2 * FL + 8, W), BF16),
-            pltpu.VMEM((Z, K, W + HD), BF16),
-            pltpu.VMEM((Z, K, W), BF16),
-            pltpu.VMEM((Z, K, W), BF16),
-            pltpu.VMEM((PL, K, W + HD), BF16),
-            pltpu.VMEM((PL, K, W), BF16),
-            pltpu.VMEM((PL, K, W), BF16),
-            pltpu.VMEM((PL, K, W + HD), BF16),
-            pltpu.VMEM((PL, K, W), BF16),
-            pltpu.VMEM((PL, K, W), BF16),
-            pltpu.VMEM((Z * K, W + HD), F32),
-            pltpu.VMEM((Z * K, W), F32),
-            pltpu.VMEM((Z * K, W), F32),
+            pltpu.VMEM((Z, 2 * K, W + HD), BF16),
+            pltpu.VMEM((Z, 2 * K, W // 2), BF16),
+            pltpu.VMEM((PL, 2 * K, W + HD), BF16),
+            pltpu.VMEM((PL, 2 * K, W // 2), BF16),
+            pltpu.VMEM((PL, 2 * K, W + HD), BF16),
+            pltpu.VMEM((PL, 2 * K, W // 2), BF16),
             pltpu.VMEM((T, K, D), F32),
             pltpu.VMEM((K, D), F32),
             pltpu.VMEM((Z, K, W), BF16),
@@ -622,11 +636,13 @@
             pltpu.VMEM((C, Y, Z * K + 8, W), BF16),
             pltpu.VMEM((Z, K, W), BF16),
             pltpu.VMEM((Z, K, W), BF16),
-            dma((18,)),
+            dma((17,)),
         ]
-        + [dma((3,))] * 7
-        + [dma(())] * 6
-        + [dma((Y,))] * 8
+        + [dma((2,))] * 9
+        + [dma(())] * 3
+        + [dma((2,))] * 3
+        + [dma((Y,))] * 4
+        + [dma((2, Y))] * 4
         + [dma(())] * 2,
         compiler_params=pltpu.CompilerParams(
             collective_id=0, has_side_effects=True, vmem_limit_bytes=60 * 1024 * 1024

time: 62.4 us -> 59.1 us (0.947)
  Pallas kernels: 60.9 us -> 57.6 us
    pallas_call x1, Pallas kernels: 60.9 us -> 57.6 us  [per_device(): pl.pallas_call(functools.partial(layer_kernel, (Z, Y, C, T, W, K)), out_s...]
where the time goes in v4:
time: 59.1 us; the launch traced here: 58.9 us
  Pallas kernels  57.6 us (97%)
  local copies, waits for them, and re-layouts  1.28 us (2%)
    pallas_call x1, Pallas kernels, per_device(): pl.pallas_call(functools.partial(layer_kernel, (Z, Y, C, T, W, K)), out_s...  57.6 us
    unnamed x1, local copies, waits for them, and re-layouts  1.28 us

profile of v4, /device:TPU:1, one launch (start us, length us, event | category | flops | bytes accessed | tf_op | source)
XLA Modules:
  0.0 58.9 jit_solution(13543310004688025269)
XLA Ops:
  0.0 57.6 %shard_map.163 = bf16[4,512]{1,0:T(4,128)(2,1)} custom-call(bf16[4,512]{1,0:T(4,128)(2,1)} %q_hbm.1, bf16[4,512]{1,0:T(4,128)(2,1)} %k_hbm.1, bf16[4,512]{1,0:T(4,128)(2,1)} %v_hbm.1, bf16[4,512]{1,0:T(4,128)(2,1)} %res_hbm.1, s32[1,512]{1,0:T(1,128)} %bitcast.7, s32[1,512]{1,0:T(1,128)} %bitcast.8, s32[1,512]{1,0:T(1,128)} %bitcast.9, s32[16,512]{1,0:T(8,128)} %bitcast.6, ...), custom_call_target="tpu_custom_call" | custom-call | tf_op jit(solution)/shard_map/pallas_call | solution.py:605
  57.6 1.3 %copy.19 = bf16[4,512]{1,0:T(4,128)(2,1)} copy(bf16[4,512]{1,0:T(4,128)(2,1)} %shard_map.163) | data formatting | bytes 8192

commit v5 on v4

--- a/solution.py
+++ b/solution.py
@@ -114,6 +114,7 @@
     ZK = Z * K
     FL = up_hbm.shape[0]
     HALF = ZK // 2
+    groups = ((0, Z // 2), (Z // 2, Z // 4), (3 * Z // 4, Z // 4))
     BLK = ZK + 8
     MID = Z // 2
     REACH = Z // 4
@@ -244,38 +245,6 @@
         BF16
     )
 
-    pl.semaphore_wait(barrier, len(near) + (PL - 1) + (T - 1))
-
-    sources = (g0, g1)
-    for n, source in enumerate(sources):
-        for d in near:
-            if abs(d) == REACH:
-                sem = low_edge_r.at[n] if d > 0 else high_edge_r.at[n]
-            else:
-                sem = low_r.at[n] if d > 0 else high_r.at[n]
-            send(source.at[MID], source.at[MID - d], near_s.at[n], sem, z_away(d))
-
-    def pass_on(n):
-        source = sources[n]
-        low, high = source.at[MID - REACH], source.at[MID + REACH]
-        drain(low, low_edge_r.at[n])
-        for e in range(REACH, 0, -1):
-            send(low, source.at[MID - REACH - e], far_s.at[n], far_r.at[n], z_away(e))
-        drain(high, high_edge_r.at[n])
-        for e in range(REACH - 1, 0, -1):
-            send(high, source.at[MID + REACH + e], far_s.at[n], far_r.at[n], z_away(-e))
-
-    for load in [loads[10], loads[11], loads[15]]:
-        load.wait()
-    spread = hot(iota((FL, W), 1) == pid * FL + iota((FL, W), 0))
-    bias8 = jnp.where(iota((8, FL), 0) == 0, vector(ub_ref), 0.0)
-    wts[pid, 2 * FL : 2 * FL + 8, :] = jnp.dot(
-        bias8.astype(BF16), spread, preferred_element_type=F32
-    ).astype(BF16)
-    for i in range(1, Y):
-        send(wts.at[pid], wts.at[pid], wy_s.at[i], wy_r.at[y], y_peer(i)[1])
-    send(wts.at[pid], wts.at[pid], wc_s.at[0], wc_r.at[y], core_peer)
-
     for load in loads[4:8]:
         load.wait()
     owner_i = meta_ref[0]
@@ -326,9 +295,41 @@
     )
     out_request = (ordered[0:1, :] * 16.0 + ordered[1:2, :]).astype(jnp.int32)
 
+
+    pl.semaphore_wait(barrier, len(near) + (PL - 1) + (T - 1))
+
+    sources = (g0, g1)
+    for n, source in enumerate(sources):
+        for d in near:
+            if abs(d) == REACH:
+                sem = low_edge_r.at[n] if d > 0 else high_edge_r.at[n]
+            else:
+                sem = low_r.at[n] if d > 0 else high_r.at[n]
+            send(source.at[MID], source.at[MID - d], near_s.at[n], sem, z_away(d))
+
+    def pass_on(n):
+        source = sources[n]
+        low, high = source.at[MID - REACH], source.at[MID + REACH]
+        drain(low, low_edge_r.at[n])
+        for e in range(REACH, 0, -1):
+            send(low, source.at[MID - REACH - e], far_s.at[n], far_r.at[n], z_away(e))
+        drain(high, high_edge_r.at[n])
+        for e in range(REACH - 1, 0, -1):
+            send(high, source.at[MID + REACH + e], far_s.at[n], far_r.at[n], z_away(-e))
+
+    for load in [loads[10], loads[11], loads[15]]:
+        load.wait()
+    spread = hot(iota((FL, W), 1) == pid * FL + iota((FL, W), 0))
+    bias8 = jnp.where(iota((8, FL), 0) == 0, vector(ub_ref), 0.0)
+    wts[pid, 2 * FL : 2 * FL + 8, :] = jnp.dot(
+        bias8.astype(BF16), spread, preferred_element_type=F32
+    ).astype(BF16)
+    for i in range(1, Y):
+        send(wts.at[pid], wts.at[pid], wy_s.at[i], wy_r.at[y], y_peer(i)[1])
+    send(wts.at[pid], wts.at[pid], wc_s.at[0], wc_r.at[y], core_peer)
+
     for n in range(2):
         pass_on(n)
-
     def to_plane(n, sendbuf, recvbuf):
         source = sources[n]
         if REACH > 1:
@@ -430,12 +431,24 @@
     loads[9].wait()
     for load in [loads[12], loads[13], loads[14], loads[16]]:
         load.wait()
-    part[t] = jnp.dot(attn, ow[...], preferred_element_type=F32)
     own1 = from_plane(1, r1)
     res_own = jnp.concatenate([own1[0:K], own1[K : 2 * K]], axis=1)
+    extra = res_own + vector(ob_ref)
+    wide_half = D // 2
+    for n in range(2):
+        cols = pl.ds(n * wide_half, wide_half)
+        add = jnp.concatenate(
+            [
+                jnp.where(t == n * (T // 2) + b, extra, 0.0)
+                for b in range(T // 2)
+            ],
+            axis=1,
+        )
+        part[t, :, cols] = jnp.dot(attn, ow[:, cols], preferred_element_type=F32) + add
+        own_part = part.at[t, :, cols]
+        for i in range(1, T):
+            send(own_part, own_part, pt_s, pt_r, tp_peer(i)[1])
     here = pl.ds(pl.multiple_of(t * W, W), W)
-    part[t, :, here] = part[t, :, here] + (res_own + vector(ob_ref))
-    each(T, lambda d: send(part.at[t], part.at[t], pt_s, pt_r, tp_peer(d)[1]))
     drain(part.at[pl.ds(0, T - 1)], pt_r)
     summed = part[0]
     for s in range(1, T):
@@ -451,8 +464,9 @@
 
     for i in range(1, Z):
         d, device = z_peer(i)
-        far = 1 if REACH < d < Z - REACH + 1 else 0
-        send(nbuf.at[REACH], nbuf.at[(REACH - d) % Z], ng_s, ng_r.at[far], device)
+        at = (REACH - d) % Z
+        group = [n for n, (first, _) in enumerate(groups) if first <= at][-1]
+        send(nbuf.at[REACH], nbuf.at[at], ng_s, ng_r.at[group], device)
 
     found = jnp.dot(
         stacked(owner_row, rank_row), hot(iota((R, KL), 0) == out_request), preferred_element_type=F32
@@ -488,15 +502,19 @@
         drain(wts.at[arrived], wc_r.at[other])
 
     up = jnp.concatenate([wts[p, 0:FL, :] for p in range(PL)], axis=0)
-    halves = (
-        (pl.ds(0, HALF), pl.ds(0, HALF + 8), pl.ds(0, HALF)),
-        (pl.ds(HALF, HALF), pl.ds(HALF + 8, HALF), pl.ds(HALF + 8, HALF)),
+    halves = tuple(
+        (
+            pl.ds(first * K, count * K),
+            pl.ds(first * K + (8 if first else 0), count * K + (0 if first else 8)),
+            pl.ds(first * K + (8 if first else 0), count * K),
+        )
+        for first, count in groups
     )
     drain(part.at[pl.ds(0, T - 1)], pt_s)
     for n, (rows_n, _, _) in enumerate(halves):
-        drain(nbuf.at[pl.ds(0, 2 * REACH - 1 + n)], ng_r.at[n])
-        first = n * (Z // 2)
-        for s in range(first, first + Z // 2):
+        first, count = groups[n]
+        drain(nbuf.at[pl.ds(0, count if first else count - 1)], ng_r.at[n])
+        for s in range(first, first + count):
             x32[s * K : (s + 1) * K, :] = nbuf[s].astype(F32)
         hidden = lax.dot_general(
             x32[rows_n, :].astype(BF16), up, (((1,), (1,)), ((), ())), preferred_element_type=F32
@@ -523,7 +541,7 @@
         active = 0.5 * before * (1.0 + lax.erf(before * math.sqrt(0.5)))
         abuf[core, y, at_n, 0 : PL * FL] = active.astype(BF16)
         if PL * FL < W:
-            abuf[core, y, at_n, PL * FL : W] = jnp.zeros((HALF, W - PL * FL), BF16)
+            abuf[core, y, at_n, PL * FL : W] = jnp.zeros(active.shape[:1] + (W - PL * FL,), BF16)
         own_block = abuf.at[core, y, sent_n]
         for i in range(1, Y):
             send(own_block, own_block, ay_s.at[n, i], ay_r.at[n, y], y_peer(i)[1])
@@ -640,9 +658,9 @@
         ]
         + [dma((2,))] * 9
         + [dma(())] * 3
-        + [dma((2,))] * 3
+        + [dma((3,))] * 3
         + [dma((Y,))] * 4
-        + [dma((2, Y))] * 4
+        + [dma((3, Y))] * 4
         + [dma(())] * 2,
         compiler_params=pltpu.CompilerParams(
             collective_id=0, has_side_effects=True, vmem_limit_bytes=60 * 1024 * 1024

time: 59.1 us -> 58.6 us (level)
  no operation moved by 1% of the time
where the time goes in v5:
time: 58.6 us; the launch traced here: 58.4 us
  Pallas kernels  57.1 us (97%)
  local copies, waits for them, and re-layouts  1.28 us (2%)
    pallas_call x1, Pallas kernels, per_device(): pl.pallas_call(functools.partial(layer_kernel, (Z, Y, C, T, W, K)), out_s...  57.1 us
    unnamed x1, local copies, waits for them, and re-layouts  1.28 us

profile of v5, /device:TPU:1, one launch (start us, length us, event | category | flops | bytes accessed | tf_op | source)
XLA Modules:
  0.0 58.4 jit_solution(18200153743908944909)
XLA Ops:
  0.0 57.1 %shard_map.163 = bf16[4,512]{1,0:T(4,128)(2,1)} custom-call(bf16[4,512]{1,0:T(4,128)(2,1)} %q_hbm.1, bf16[4,512]{1,0:T(4,128)(2,1)} %k_hbm.1, bf16[4,512]{1,0:T(4,128)(2,1)} %v_hbm.1, bf16[4,512]{1,0:T(4,128)(2,1)} %res_hbm.1, s32[1,512]{1,0:T(1,128)} %bitcast.7, s32[1,512]{1,0:T(1,128)} %bitcast.8, s32[1,512]{1,0:T(1,128)} %bitcast.9, s32[16,512]{1,0:T(8,128)} %bitcast.6, ...), custom_call_target="tpu_custom_call" | custom-call | tf_op jit(solution)/shard_map/pallas_call | solution.py:623
  57.1 1.3 %copy.19 = bf16[4,512]{1,0:T(4,128)(2,1)} copy(bf16[4,512]{1,0:T(4,128)(2,1)} %shard_map.163) | data formatting | bytes 8192

commit v6 on v5

--- a/solution.py
+++ b/solution.py
@@ -544,14 +544,19 @@
             abuf[core, y, at_n, PL * FL : W] = jnp.zeros(active.shape[:1] + (W - PL * FL,), BF16)
         own_block = abuf.at[core, y, sent_n]
         for i in range(1, Y):
-            send(own_block, own_block, ay_s.at[n, i], ay_r.at[n, y], y_peer(i)[1])
+            other, device = y_peer(i)
+            send(own_block, own_block, ay_s.at[n, i], ay_r.at[n, y], device)
+            if n == len(halves) - 1:
+                twin = {"req": z * PL + other * C + (1 - core)}
+                send(own_block, own_block, ac_s.at[n, i], ac_r.at[n, y], twin)
         send(own_block, own_block, ac_s.at[n, 0], ac_r.at[n, y], core_peer)
     for n, (_, sent_n, _) in enumerate(halves):
         for i in range(Y - 1, 0, -1):
             other, _ = y_peer(i)
             block_n = abuf.at[core, other, sent_n]
             drain(block_n, ay_r.at[n, other])
-            send(block_n, block_n, ac_s.at[n, i], ac_r.at[n, other], core_peer)
+            if n < len(halves) - 1:
+                send(block_n, block_n, ac_s.at[n, i], ac_r.at[n, other], core_peer)
     for n, (_, sent_n, _) in enumerate(halves):
         for s in range(Y):
             drain(abuf.at[1 - core, s, sent_n], ac_r.at[n, s])

time: 58.6 us -> 58.4 us (level)
  no operation moved by 1% of the time
where the time goes in v6:
time: 58.4 us; the launch traced here: 58.3 us
  Pallas kernels  57 us (98%)
  local copies, waits for them, and re-layouts  1.28 us (2%)
    pallas_call x1, Pallas kernels, per_device(): pl.pallas_call(functools.partial(layer_kernel, (Z, Y, C, T, W, K)), out_s...  57 us
    unnamed x1, local copies, waits for them, and re-layouts  1.28 us

profile of v6, /device:TPU:1, one launch (start us, length us, event | category | flops | bytes accessed | tf_op | source)
XLA Modules:
  0.0 58.3 jit_solution(16809297427858310559)
XLA Ops:
  0.0 57.0 %shard_map.163 = bf16[4,512]{1,0:T(4,128)(2,1)} custom-call(bf16[4,512]{1,0:T(4,128)(2,1)} %q_hbm.1, bf16[4,512]{1,0:T(4,128)(2,1)} %k_hbm.1, bf16[4,512]{1,0:T(4,128)(2,1)} %v_hbm.1, bf16[4,512]{1,0:T(4,128)(2,1)} %res_hbm.1, s32[1,512]{1,0:T(1,128)} %bitcast.7, s32[1,512]{1,0:T(1,128)} %bitcast.8, s32[1,512]{1,0:T(1,128)} %bitcast.9, s32[16,512]{1,0:T(8,128)} %bitcast.6, ...), custom_call_target="tpu_custom_call" | custom-call | tf_op jit(solution)/shard_map/pallas_call | solution.py:628
  57.0 1.3 %copy.19 = bf16[4,512]{1,0:T(4,128)(2,1)} copy(bf16[4,512]{1,0:T(4,128)(2,1)} %shard_map.163) | data formatting | bytes 8192
